TPU v7x, 32 devices: a whole 2x2x4 slice. The times are simulated.
32 devices in a mesh: section: 2 (over x), dp: 16 (over z, y, core).
Axes of the slice: x: 2, y: 2, z: 4, core: 2. Of those that a mesh axis runs over, the one named last changes fastest.
Arguments:
- inputs_long: bfloat16 [2, 16, 640, 768], P('section', 'dp'), may hold values from -6 to 6
- inputs_short: bfloat16 [2, 16, 256, 768], P('section', 'dp'), may hold values from -6 to 6
- cotangent_long: bfloat16 [2, 16, 640, 768], P('section', 'dp'), may hold values from -6 to 6
- cotangent_short: bfloat16 [2, 16, 256, 768], P('section', 'dp'), may hold values from -6 to 6
- lengths_long: int32 [2, 16], P(None, 'dp'), may hold values from 1 to 640, 7680 in all within a row
- lengths_short: int32 [2, 16], P(None, 'dp'), may hold values from 1 to 256, 3072 in all within a row
- self_in_weight: bfloat16 [2, 768, 2304], P('section'), may hold values from -0.3125 to 0.3125
- self_out_weight: bfloat16 [2, 768, 768], P('section'), may hold values from -0.625 to 0.625
- expand_weight: bfloat16 [2, 768, 3072], P('section'), may hold values from -0.21875 to 0.21875
- contract_weight: bfloat16 [2, 3072, 768], P('section'), may hold values from -0.109375 to 0.109375
- expand_bias: float32 [2, 3072], P('section'), may hold values from -1.75 to 1.75
- layer_biases: float32 [2, 6, 768], P('section'), may hold values from -1.75 to 1.75
- layer_gains: float32 [2, 2, 768], P('section'), may hold values from 0.25 to 1.75
- cross_weight: bfloat16 [768, 3072], replicated, may hold values from -0.3125 to 0.3125
- cross_biases: float32 [4, 768], replicated, may hold values from -1.75 to 1.75
- cross_gain: float32 [768], replicated, may hold values from 0.25 to 1.75
Outputs:
- outputs_long: bfloat16 [2, 16, 640, 768], P('section', 'dp')
- outputs_short: bfloat16 [2, 16, 256, 768], P('section', 'dp')
- input_grad_long: float32 [2, 16, 640, 768], P('section', 'dp')
- input_grad_short: float32 [2, 16, 256, 768], P('section', 'dp')
- self_in_grad: float32 [2, 768, 2304], P('section', 'dp')
- self_out_grad: float32 [2, 768, 768], P('section', 'dp')
- expand_grad: float32 [2, 768, 3072], P('section', 'dp')
- contract_grad: float32 [2, 3072, 768], P('section', 'dp')
- expand_bias_grad: float32 [2, 3072], P('section', 'dp')
- bias_grad: float32 [2, 6, 768], P('section', None, 'dp')
- gain_grad: float32 [2, 2, 768], P('section', None, 'dp')
- cross_grad: float32 [768, 3072], P(None, ('section', 'dp'))
- cross_bias_grad: float32 [4, 768], replicated
- cross_gain_grad: float32 [768], replicated
Inputs may be any that keep to these rules, and one draw needn't show every extreme that they name: In each row of lengths_long the lengths sum to 7680 and the largest is 640. In each row of lengths_short the lengths sum to 3072 and the largest is 256.
All inputs are finite; a program needn't handle non-finite values. No bound on the sum of `lengths_long` or of `lengths_short` on one device may be relied on, other than what follows from the above.
Results may differ from a plain program's by a relative error of at most 0.02.
Values may be sent and summed in bfloat16 or wider, within the bound.
A program may use at most 320 MiB of HBM per device.

v0:
```python
import functools
import jax
import jax.numpy as jnp
from jax import lax
from jax.experimental import pallas as pl
from jax.experimental.pallas import tpu as pltpu
from jax.sharding import PartitionSpec as P

BF, F32 = jnp.bfloat16, jnp.float32
NEG = -1e30
NT = (((1,), (1,)), ((), ()))
TN = (((0,), (0,)), ((), ()))

def dot(a, b):
    return jnp.dot(a, b, preferred_element_type=F32)
def dot_nt(a, b):
    return lax.dot_general(a, b, NT, preferred_element_type=F32)
def dot_tn(a, b):
    return lax.dot_general(a, b, TN, preferred_element_type=F32)

def lanes(rows):
    return lax.broadcasted_iota(jnp.int32, (rows, 128), 1)

def split3(v):
    hi = v.astype(BF)
    rest = v - hi.astype(F32)
    mid = rest.astype(BF)
    low = (rest - mid.astype(F32)).astype(BF)
    return hi, mid, low

def blank(*shapes):
    def nothing(*refs):
        pass

    return pl.pallas_call(
        nothing,
        out_shape=[jax.ShapeDtypeStruct(shape, kind) for shape, kind in shapes],
        out_specs=[pl.BlockSpec(memory_space=pl.ANY)] * len(shapes),
    )()


def norm_forward(u, gain, shift):
    mean = jnp.mean(u, axis=-1, keepdims=True)
    c = u - mean
    r = lax.rsqrt(jnp.mean(c * c, axis=-1, keepdims=True) + 1e-5)
    xhat = c * r
    return xhat, r, xhat * gain + shift

def causal_shift(size):
    return jnp.where(lax.axis_index("section") == 1, 0, size)


def attn_fwd_kernel(same, len_ref, xq_ref, xkv_ref, res_ref, wqkv_ref, wo_ref, bias_ref, gain_ref,
                    qkv_ref, o_ref, lse_ref, xhat_ref, r_ref, n_ref):
    s, d = xq_ref.shape
    if not same:
        wo_ref = wqkv_ref.at[:, 3 * d :]
    xq = xq_ref[...].astype(BF)
    xkv = xq if same else xkv_ref[...]
    qkv_ref[:, :d] = (dot(xq, wqkv_ref[:, :d]) + bias_ref[0:1, :]).astype(BF)
    qkv_ref[:, d:2*d] = dot(xkv, wqkv_ref[:, d:2*d]).astype(BF)
    qkv_ref[:, 2*d:] = (dot(xkv, wqkv_ref[:, 2*d:3*d]) + bias_ref[1:2, :]).astype(BF)
    length = len_ref[0, 0]
    lane = lanes(s)
    row = lax.broadcasted_iota(jnp.int32, (s, 128), 0)
    key_bias = jnp.where(row < length, 0.0, NEG).astype(BF)
    if same:
        tri = lax.broadcasted_iota(jnp.int32, (s, s), 1) <= lax.broadcasted_iota(jnp.int32, (s, s), 0) + causal_shift(s)
    one = jnp.ones((s, 128), BF)
    zero = jnp.zeros((s, 128), BF)

    def pair(p, _):
        at = pl.multiple_of(p * 128, 128)
        q = qkv_ref[:, pl.ds(at, 128)] * jnp.asarray(0.125, BF)
        k = qkv_ref[:, pl.ds(d + at, 128)]
        v = qkv_ref[:, pl.ds(2 * d + at, 128)]
        outs, lses = [], []
        for h in range(2):
            mine = (lane < 64) if h == 0 else (lane >= 64)
            other = 64 if h == 0 else 0
            qh = jnp.where(mine, q, jnp.where(lane == other, one, zero))
            kh = jnp.where(mine, k, jnp.where(lane == other, key_bias, zero))
            sc = dot_nt(qh, kh)
            if same:
                sc = jnp.where(tri, sc, NEG)
            m = jnp.max(sc, axis=-1, keepdims=True)
            e = jnp.exp(sc - m)
            l = jnp.sum(e, axis=-1, keepdims=True)
            outs.append(dot(e.astype(BF), v) * (1.0 / l))
            lses.append(m + jnp.log(l))
        o_ref[:, pl.ds(at, 128)] = jnp.where(lane < 64, outs[0], outs[1]).astype(BF)
        lse_ref[:, pl.ds(at, 128)] = jnp.where(lane < 64, lses[1], lses[0])
        return 0
    lax.fori_loop(0, d // 128, pair, 0)
    u = res_ref[...].astype(F32) + dot(o_ref[...], wo_ref[...]) + bias_ref[2:3, :]
    xhat, r, n = norm_forward(u, gain_ref[0:1, :], bias_ref[3:4, :])
    xhat_ref[...] = xhat
    r_ref[...] = jnp.broadcast_to(r, r_ref.shape)
    n_ref[...] = n

def attn_fwd(xq, xkv, res, wqkv, wo, bias, gain, length):
    s, d = xq.shape
    same = xkv is None
    if same:
        xkv = xq
    else:
        wo = gain
    vm = pl.BlockSpec(memory_space=pltpu.VMEM)
    sm = pl.BlockSpec(memory_space=pltpu.SMEM)
    return pl.pallas_call(
        functools.partial(attn_fwd_kernel, same),
        out_shape=(jax.ShapeDtypeStruct((s, 3 * d), BF), jax.ShapeDtypeStruct((s, d), BF), jax.ShapeDtypeStruct((s, d), F32),
                   jax.ShapeDtypeStruct((s, d), F32), jax.ShapeDtypeStruct((s, 128), F32), jax.ShapeDtypeStruct((s, d), F32)),
        in_specs=[sm] + [vm] * 7, out_specs=(vm,) * 6,
        compiler_params=pltpu.CompilerParams(vmem_limit_bytes=60 << 20),
    )(length.reshape(1, 1), xq, xkv, res, wqkv, wo, bias, gain)

def norm_backward(dn, xhat, r, gain):
    h = dn * gain
    return r * (h - jnp.mean(h, axis=-1, keepdims=True) - xhat * jnp.mean(h * xhat, axis=-1, keepdims=True))

def attn_bwd_body(same, between, len_ref, dn_ref, qkv_ref, o_ref, lse_ref, xhat_ref, r_ref, wqkv_ref, wo_ref, gain_ref,
                  dres_ref, dqkv_ref, dt_ref, dkvx_ref, sums_ref, do_ref, dq_ref):
    s, d = dn_ref.shape
    if not same:
        wo_ref = wqkv_ref.at[:, 3 * d :]
    dn = dn_ref[...]
    xhat = xhat_ref[...]
    du = norm_backward(dn, xhat, r_ref[:, :1], gain_ref[0:1, :])
    dt = du.astype(BF)
    dt_ref[...] = dt
    sums_ref[2:3, :] = jnp.sum(dt.astype(F32), axis=0, keepdims=True)
    sums_ref[3:4, :] = jnp.sum(dn, axis=0, keepdims=True)
    sums_ref[4:5, :] = jnp.sum(dn * xhat, axis=0, keepdims=True)
    dres_ref[...] = du
    do_ref[...] = dot_nt(dt, wo_ref[...]).astype(BF)
    length = len_ref[0, 0]
    lane = lanes(s)
    row = lax.broadcasted_iota(jnp.int32, (s, 128), 0)
    key_bias = jnp.where(row < length, 0.0, NEG).astype(BF)
    if same:
        tri = lax.broadcasted_iota(jnp.int32, (s, s), 0) <= lax.broadcasted_iota(jnp.int32, (s, s), 1) + causal_shift(s)
    one = jnp.ones((s, 128), BF)
    zero = jnp.zeros((s, 128), BF)

    def place(base, mine, other, extra):
        out = zero
        for j, val in enumerate(extra):
            out = jnp.where(lane == other + j, val, out)
        return jnp.where(mine, base, out)

    def pair(p, _):
        between(p)
        at = pl.multiple_of(p * 128, 128)
        q = qkv_ref[:, pl.ds(at, 128)] * jnp.asarray(0.125, BF)
        k = qkv_ref[:, pl.ds(d + at, 128)]
        v = qkv_ref[:, pl.ds(2 * d + at, 128)]
        do = do_ref[:, pl.ds(at, 128)]
        lse3 = split3(-lse_ref[:, pl.ds(at, 128)])
        prod = do.astype(F32) * o_ref[:, pl.ds(at, 128)].astype(F32)
        dq, dk, dv = [], [], []
        for h in range(2):
            mine = (lane < 64) if h == 0 else (lane >= 64)
            other = 64 if h == 0 else 0
            inner = jnp.broadcast_to(jnp.sum(jnp.where(mine, prod, 0.0), axis=-1, keepdims=True), (s, 128))
            qh = place(q, mine, other, (*lse3, one))
            kh = place(k, mine, other, (one, one, one, key_bias))
            doh = place(do, mine, other, split3(-inner))
            vh = place(v, mine, other, (one, one, one))
            st = dot_nt(kh, qh)
            if same:
                st = jnp.where(tri, st, NEG)
            pt = jnp.exp(st)
            dst = (pt * dot_nt(vh, doh)).astype(BF)
            dv.append(dot(pt.astype(BF), do))
            dk.append(dot(dst, q))
            dq.append(dot_tn(k, dst))
        m1 = lane < 64
        dq_ref[...] = jnp.where(lax.broadcasted_iota(jnp.int32, (128, s), 0) < 64, dq[0], dq[1])
        dqkv_ref[:, pl.ds(at, 128)] = (dq_ref[...].T * 0.125).astype(BF)
        dqkv_ref[:, pl.ds(d + at, 128)] = jnp.where(m1, dk[0], dk[1]).astype(BF)
        dqkv_ref[:, pl.ds(2 * d + at, 128)] = jnp.where(m1, dv[0], dv[1]).astype(BF)
        return 0
    lax.fori_loop(0, d // 128, pair, 0)
    if same:
        dres_ref[...] += dot_nt(dqkv_ref[...], wqkv_ref[...])
    else:
        dres_ref[...] += dot_nt(dqkv_ref[:, :d], wqkv_ref[:, :d])
        dkvx_ref[...] = dot_nt(dqkv_ref[:, d:], wqkv_ref[:, d:3*d]).astype(BF)
    sums_ref[0:1, :] = jnp.sum(dqkv_ref[:, :d].astype(F32), axis=0, keepdims=True)
    sums_ref[1:2, :] = jnp.sum(dqkv_ref[:, 2*d:].astype(F32), axis=0, keepdims=True)
    sums_ref[5:8, :] = jnp.zeros((3, d), F32)

def attn_bwd_kernel(same, *refs):
    attn_bwd_body(same, lambda p: None, *refs)


def attn_bwd(dn, saved, wqkv, wo, gain, length, same):
    qkv, o, lse, xhat, r = saved
    s, d = dn.shape
    if not same:
        wo = gain
    vm = pl.BlockSpec(memory_space=pltpu.VMEM)
    sm = pl.BlockSpec(memory_space=pltpu.SMEM)
    return pl.pallas_call(
        functools.partial(attn_bwd_kernel, same),
        out_shape=(jax.ShapeDtypeStruct((s, d), F32), jax.ShapeDtypeStruct((s, 3 * d), BF), jax.ShapeDtypeStruct((s, d), BF),
                   jax.ShapeDtypeStruct((8, 128) if same else (s, d), BF), jax.ShapeDtypeStruct((8, d), F32)),
        in_specs=[sm] + [vm] * 9, out_specs=(vm,) * 5,
        scratch_shapes=[pltpu.VMEM((s, d), BF), pltpu.VMEM((128, s), F32)],
        compiler_params=pltpu.CompilerParams(vmem_limit_bytes=60 << 20),
    )(length.reshape(1, 1), dn, qkv, o, lse, xhat, r, wqkv, wo, gain)

def gelu_parts(a):
    e = jnp.exp(-0.5 * a * a)
    t = 1.0 / (1.0 + 0.23164188624 * jnp.abs(a))
    tail = t * (0.127414796 + t * (-0.142248368 + t * (0.7107068705 + t * (-0.7265760135 + t * 0.5307027145)))) * e
    phi_cap = jnp.where(a < 0.0, tail, 1.0 - tail)
    return phi_cap, e * 0.3989422804014327

def ffn_fwd_kernel(n_ref, we_ref, wc_ref, be_ref, bias_ref, gain_ref,
                   y_ref, g_ref, gp_ref, xhat_ref, r_ref, acc_ref, low_ref):
    @pl.when(pl.program_id(0) == 0)
    def _():
        low_ref[...] = n_ref[...].astype(BF)
        acc_ref[...] = n_ref[...] + bias_ref[4:5, :]

    a = dot(low_ref[...], we_ref[...]) + be_ref[...]
    cap, dens = gelu_parts(a)
    g = (a * cap).astype(BF)
    g_ref[...] = g
    gp_ref[...] = (cap + a * dens).astype(BF)
    acc_ref[...] += dot(g, wc_ref[...])

    @pl.when(pl.program_id(0) == pl.num_programs(0) - 1)
    def _():
        xhat, r, y = norm_forward(acc_ref[...], gain_ref[1:2, :], bias_ref[5:6, :])
        xhat_ref[...] = xhat
        r_ref[...] = jnp.broadcast_to(r, r_ref.shape)
        y_ref[...] = y.astype(BF)


def whole(*shape):
    return pl.BlockSpec(shape, lambda c: (0, 0))


def ffn_fwd(n, we, wc, be, bias, gain, chunk=768):
    s, d = n.shape
    ff = we.shape[1]
    columns = pl.BlockSpec((s, chunk), lambda c: (0, c))
    return pl.pallas_call(
        ffn_fwd_kernel,
        out_shape=(jax.ShapeDtypeStruct((s, d), BF), jax.ShapeDtypeStruct((s, ff), BF), jax.ShapeDtypeStruct((s, ff), BF),
                   jax.ShapeDtypeStruct((s, d), F32), jax.ShapeDtypeStruct((s, 128), F32)),
        grid=(ff // chunk,),
        in_specs=[whole(s, d), pl.BlockSpec((d, chunk), lambda c: (0, c)), pl.BlockSpec((chunk, d), lambda c: (c, 0)),
                  pl.BlockSpec((1, chunk), lambda c: (0, c)), whole(*bias.shape), whole(*gain.shape)],
        out_specs=(whole(s, d), columns, columns, whole(s, d), whole(s, 128)),
        scratch_shapes=[pltpu.VMEM((s, d), F32), pltpu.VMEM((s, d), BF)],
        compiler_params=pltpu.CompilerParams(vmem_limit_bytes=60 << 20),
    )(n, we, wc, be.reshape(1, ff), bias, gain)


def ffn_bwd_kernel(extra, len_ref, cot_ref, dm_ref, gp_ref, xhat_ref, r_ref, we_ref, wc_ref, gain_ref,
                   dn_ref, da_ref, dt_ref, sums_ref, sume_ref):
    s, d = cot_ref.shape

    @pl.when(pl.program_id(0) == 0)
    def _():
        row = lax.broadcasted_iota(jnp.int32, (s, 1), 0)
        dy = jnp.where(row < len_ref[0, 0], cot_ref[...].astype(F32), 0.0)
        if extra:
            dy = dy + dm_ref[...].astype(F32)
        xhat = xhat_ref[...]
        du = norm_backward(dy, xhat, r_ref[:, :1], gain_ref[1:2, :])
        dt = du.astype(BF)
        dt_ref[...] = dt
        sums_ref[0:1, :] = jnp.sum(dt.astype(F32), axis=0, keepdims=True)
        sums_ref[1:2, :] = jnp.sum(dy, axis=0, keepdims=True)
        sums_ref[2:3, :] = jnp.sum(dy * xhat, axis=0, keepdims=True)
        sums_ref[3:8, :] = jnp.zeros((5, d), F32)
        dn_ref[...] = du

    dg = dot_nt(dt_ref[...], wc_ref[...])
    da = (dg * gp_ref[...].astype(F32)).astype(BF)
    da_ref[...] = da
    sume_ref[...] = jnp.sum(da.astype(F32), axis=0, keepdims=True)
    dn_ref[...] += dot_nt(da, we_ref[...])


def ffn_bwd(cot, dm, length, saved, we, wc, gain, chunk=768):
    gp, xhat, r = saved
    s, d = cot.shape
    ff = we.shape[1]
    extra = dm is not None
    sm = pl.BlockSpec(memory_space=pltpu.SMEM)
    columns = pl.BlockSpec((s, chunk), lambda c: (0, c))
    row = pl.BlockSpec((1, chunk), lambda c: (0, c))
    if not extra:
        dm = cot[:8]
    return pl.pallas_call(
        functools.partial(ffn_bwd_kernel, extra),
        out_shape=(jax.ShapeDtypeStruct((s, d), F32), jax.ShapeDtypeStruct((s, ff), BF), jax.ShapeDtypeStruct((s, d), BF),
                   jax.ShapeDtypeStruct((8, d), F32), jax.ShapeDtypeStruct((1, ff), F32)),
        grid=(ff // chunk,),
        in_specs=[sm, whole(s, d), whole(*dm.shape), columns, whole(s, d), whole(s, 128),
                  pl.BlockSpec((d, chunk), lambda c: (0, c)), pl.BlockSpec((chunk, d), lambda c: (c, 0)),
                  whole(*gain.shape)],
        out_specs=(whole(s, d), columns, whole(s, d), whole(8, d), row),
        compiler_params=pltpu.CompilerParams(vmem_limit_bytes=60 << 20),
    )(length.reshape(1, 1), cot, dm, gp, xhat, r, we, wc, gain)


MESH = pl.DeviceIdType.MESH
LAG = 2
RING = 8


def store_rows(total, out_ref):
    blocks, shards, rows, width = out_ref.shape
    halves = total.shape[1] // width
    groups = blocks // halves
    for k in range(shards):
        for j in range(groups):
            at = (k * groups + j) * rows
            for h in range(halves):
                out_ref[j * halves + h, k] = total[at : at + rows, h * width : (h + 1) * width]


def product(xs, dys):
    total = None
    for x, dy in zip(xs, dys):
        part = dot_tn(x[...].astype(BF), dy[...].astype(BF))
        total = part if total is None else total + part
    return total.astype(BF)


def wgrad_rows_kernel(n, *refs):
    store_rows(product(refs[:n], refs[n : 2 * n]), refs[2 * n])


def wgrad_rows(xs, dys, shards):
    sizes = [x.shape[0] for x in xs]
    n, k = xs[0].shape[1], dys[0].shape[1]
    width, rows = k // 2, k // shards
    groups = n // k
    return pl.pallas_call(
        functools.partial(wgrad_rows_kernel, len(xs)),
        out_shape=jax.ShapeDtypeStruct((2 * groups, shards, rows, width), BF),
        grid=(n // k,),
        in_specs=[pl.BlockSpec((s, k), lambda i: (0, i)) for s in sizes]
        + [pl.BlockSpec((s, k), lambda i: (0, 0)) for s in sizes],
        out_specs=pl.BlockSpec((2 * groups, shards // groups, rows, width), lambda i: (0, i, 0, 0)),
        compiler_params=pltpu.CompilerParams(vmem_limit_bytes=60 << 20),
    )(*xs, *dys)


def wgrad_cross_kernel(n, *refs):
    dqkv, dt, n1, mem, mixed = (refs[j * n : (j + 1) * n] for j in range(5))
    first_ref, second_ref = refs[5 * n :]
    i = pl.program_id(0)
    for at, xs, dys, out_ref in (
        (0, dqkv, n1, first_ref),
        (1, dqkv, mem, first_ref),
        (2, dqkv, mem, second_ref),
        (3, dt, mixed, second_ref),
    ):

        @pl.when(i == at)
        def _():
            store_rows(product(xs, dys), out_ref)


def wgrad_cross(dqkv, dt, n1, mem, mixed, shards):
    sizes = [x.shape[0] for x in dt]
    k = dt[0].shape[1]
    width, rows = k // 2, k // shards
    out = jax.ShapeDtypeStruct((4, shards, rows, width), BF)
    whole = [pl.BlockSpec((s, k), lambda i: (0, 0)) for s in sizes]
    return pl.pallas_call(
        functools.partial(wgrad_cross_kernel, len(sizes)),
        out_shape=(out, out),
        grid=(4,),
        in_specs=[pl.BlockSpec((s, k), lambda i: (0, jnp.minimum(i, 2))) for s in sizes] + whole * 4,
        out_specs=(
            pl.BlockSpec((4, shards // 2, rows, width), lambda i: (0, jnp.minimum(i, 1), 0, 0)),
            pl.BlockSpec((4, shards // 2, rows, width), lambda i: (0, jnp.maximum(i - 2, 0), 0, 0)),
        ),
        compiler_params=pltpu.CompilerParams(vmem_limit_bytes=60 << 20),
    )(*dqkv, *dt, *n1, *mem, *mixed)


def reduce_kernel(counts, *refs):
    (len_ref, dn_ref, qkv_ref, o_ref, lse_ref, xhat_ref, r_ref, wqkv_ref, wo_ref, gain_ref) = refs[:10]
    (x0_ref, x_ref, dqkv0_ref, o0_ref, dt0_ref, contract, cross_first, cross_second) = refs[10:18]
    ffn_refs = (refs[18:22], refs[22:26])
    (ssum_ref, fsum_ref, esum_ref, csum_ref) = refs[26:30]
    (dres_ref, in_ref, out_ref, expand_ref, contract_ref, cross_ref, vsum_ref, landed) = refs[30:38]
    (dqkv_ref, dt_ref, do_ref, dq_ref, sums_ref, made, own, r0, r1, r2, r3, vbuf, vrecv) = refs[38:51]
    (n0_buf, n1_buf, da0_buf, da1_buf) = refs[51:55]
    send_sem, recv_sem, local_sem, vsend_sem, vrecv_sem, xsend_sem, xrecv_sem, fetch_sem = refs[55:]
    d = dn_ref.shape[1]
    n_ffn, n_in, n_out, n_cross = 2 * counts[0], counts[1], counts[2], counts[3]
    blocks = n_ffn + n_in + n_out + n_cross
    rows, width = own.shape[-2:]
    second = lax.axis_index("section") == 1
    me = lax.axis_index("dp")
    c, y, zl, zh = me % 2, (me // 2) % 2, (me // 4) % 2, me // 8
    mates = (me + 1 - 2 * c, me + 2 - 4 * y, me + 4 - 8 * zl, me + 8 - 16 * zh)
    barrier = pltpu.get_barrier_semaphore()
    for mate in mates:
        pl.semaphore_signal(barrier, inc=1, device_id={"dp": mate}, device_id_type=MESH)
    across = 1 - lax.axis_index("section")
    pl.semaphore_signal(barrier, inc=1, device_id={"section": across}, device_id_type=MESH)

    def chosen(visit):
        for which, here in enumerate((jnp.logical_not(second), second)):

            @pl.when(here)
            def _():
                visit(ffn_refs[which])

    def fetch_norms(from_refs):
        return [
            pltpu.make_async_copy(from_refs[k], (n0_buf, n1_buf)[k], fetch_sem.at[2, k]) for k in range(2)
        ]

    def fetch_columns(from_refs, i):
        at = pl.ds(pl.multiple_of(i * d, 128), d)
        return [
            pltpu.make_async_copy(
                from_refs[2 + k].at[:, at], (da0_buf, da1_buf)[k].at[i % 2], fetch_sem.at[i % 2, k]
            )
            for k in range(2)
        ]

    def begin_fetch(from_refs):
        for copy in fetch_norms(from_refs) + fetch_columns(from_refs, 0) + fetch_columns(from_refs, 1):
            copy.start()

    chosen(begin_fetch)
    pl.semaphore_wait(barrier, 5)

    def over(j):
        return pltpu.make_async_remote_copy(
            src_ref=cross_first.at[j],
            dst_ref=landed.at[j],
            send_sem=xsend_sem.at[j],
            recv_sem=xrecv_sem.at[j],
            device_id={"section": across},
            device_id_type=MESH,
        )

    @pl.when(second)
    def _():
        for j in (*range(n_cross // 2, n_cross), *range(n_cross // 2)):
            over(j).start()

    order = ((0, 1, 2, 3), (0, 2, 3, 1))

    def remote(src, dst, stage, b, color):
        return pltpu.make_async_remote_copy(
            src_ref=src,
            dst_ref=dst,
            send_sem=send_sem.at[stage, b],
            recv_sem=recv_sem.at[stage, b],
            device_id={"dp": mates[order[color][stage]]},
            device_id_type=MESH,
        )

    turned = blocks // 7
    half = turned // 2
    steps = blocks - turned
    gap = 3
    early = counts[0] - half

    def slot(b, color):
        if color == 0:
            return (b - jnp.where(b >= early, half, 0)) % RING
        return RING + jnp.where(b < steps, b - early, b - steps)

    def first_copy(part, at, b, color):
        return remote(part.at[at, :, :, :, 1 - c], r0.at[slot(b, color)], 0, b, color)

    def local_copy(part, at, b):
        return pltpu.make_async_copy(part.at[at, :, :, :, c], own.at[b], local_sem.at[b])

    def copy_of(stage, b, color):
        if color == 0:
            src = (own.at[b, :, :, 1 - y], own.at[b, :, 1 - zl, y], own.at[b, 1 - zh, zl, y])
        else:
            src = (own.at[b, :, 1 - zl], own.at[b, 1 - zh, zl], own.at[b, zh, zl, 1 - y])
        return remote(src[stage - 1], (r1, r2, r3)[stage - 1].at[b], stage, b, color)

    def add(left, right):
        return (left.astype(F32) + right.astype(F32)).astype(BF)

    def column(at):
        return pl.ds(pl.multiple_of(at * width, 128), width)

    def put_columns(ref, at, value):
        ref[:, column(at)] = value

    def put_groups(ref, at, value):
        ref[pl.ds(pl.multiple_of((at // 2) * rows, 8), rows), column(at % 2)] = value

    plan = (
        (((contract, None),), counts[0], put_groups, contract_ref),
        (((made, None),), counts[0], put_columns, expand_ref),
        (((made, None),), n_in, put_columns, in_ref),
        (((made, None),), n_out, put_columns, out_ref),
        (((landed, jnp.logical_not(second)), (cross_second, second)), n_cross, put_groups, cross_ref),
    )

    def each(b, visit):
        low = 0
        for sources, count, put, target in plan:
            inside = (b >= low) & (b < low + count)
            at = b % counts[0] if sources[0][0] is made else b - low
            visit(inside, sources, at, put, target, b - low)
            low += count

    def settle(stage, b, color):
        if stage == 0:
            first_copy(contract, 0, b, color).wait()
            local_copy(contract, 0, b).wait()
            own[b] = add(own[b], r0[slot(b, color)])
            return
        copy_of(stage, b, color).wait()
        if stage == 1:
            if color == 0:
                own[b, :, :, y] = add(own[b, :, :, y], r1[b])
            else:
                own[b, :, zl] = add(own[b, :, zl], r1[b])
        elif stage == 2:
            if color == 0:
                own[b, :, zl, y] = add(own[b, :, zl, y], r2[b])
            else:
                own[b, zh, zl] = add(own[b, zh, zl], r2[b])
        else:
            total = own[b, zh, zl, y].astype(F32) + r3[b].astype(F32)

            def finish(inside, sources, at, put, target, place):
                @pl.when(inside)
                def _():
                    put(target, place, total)

            each(b, finish)

    def vcopy(j):
        return pltpu.make_async_remote_copy(
            src_ref=vbuf.at[j],
            dst_ref=vrecv.at[j],
            send_sem=vsend_sem.at[j],
            recv_sem=vrecv_sem.at[j],
            device_id={"dp": mates[j]},
            device_id_type=MESH,
        )

    def advance(stage, b, color):
        if stage == 0:

            def launch(inside, sources, at, put, target, place):
                for part, here in sources:

                    @pl.when(inside if here is None else inside & here)
                    def _():
                        if part is landed:
                            over(at).wait_recv()
                        first_copy(part, at, b, color).start()
                        local_copy(part, at, b).start()

            each(b, launch)
            return
        settle(stage - 1, b, color)
        if stage < 4:
            copy_of(stage, b, color).start()

    def step(it, _):
        for stage in range(5):
            at = it - LAG * stage

            @pl.when((at >= 0) & (at < steps))
            def _():
                advance(stage, at + jnp.where(at >= early, half, 0), 0)

            @pl.when((at >= 0) & (at < turned * gap) & (at % gap == 1))
            def _():
                j = at // gap
                advance(stage, jnp.where(j < half, early, steps) + j, 1)

        return 0

    def some(low, high):
        lax.fori_loop(low, high, step, 0)

    def keep(block, total):
        for h in range(2):
            made[block + h] = total[:, h * width : (h + 1) * width].reshape(made.shape[1:]).astype(BF)

    pairs, chunks = d // 128, counts[0] // 2

    def beside(p):
        @pl.when(p < chunks)
        def _():
            @pl.when(p == 0)
            def _():
                for copy in fetch_norms(ffn_refs[0]):
                    copy.wait()

            for copy in fetch_columns(ffn_refs[0], p):
                copy.wait()
            keep(
                2 * p,
                dot_tn(n0_buf[...].astype(BF), da0_buf[p % 2]) + dot_tn(n1_buf[...].astype(BF), da1_buf[p % 2]),
            )

            def next_fetch(from_refs):
                for copy in fetch_columns(from_refs, p + 2):
                    copy.start()

            @pl.when(p + 2 < chunks)
            def _():
                chosen(next_fetch)

        some(jnp.minimum(3 + 2 * p, 7 + p), jnp.minimum(5 + 2 * p, 8 + p))

    some(0, 3)
    attn_bwd_body(
        True, beside,
        len_ref, dn_ref, qkv_ref, o_ref, lse_ref, xhat_ref, r_ref, wqkv_ref, wo_ref, gain_ref,
        dres_ref, dqkv_ref, dt_ref, None, sums_ref, do_ref, dq_ref,
    )
    after = 7 + pairs
    vbuf[0, 0:4] = sums_ref[0:4, :] + ssum_ref[0:4, :]
    vbuf[0, 4:6] = fsum_ref[0:2, :]
    vbuf[0, 6:7] = sums_ref[4:5, :] + ssum_ref[4:5, :]
    vbuf[0, 7:8] = fsum_ref[2:3, :]
    count = esum_ref.shape[1] // d
    for j in range(count):
        vbuf[0, 8 + j : 9 + j] = esum_ref[:, j * d : (j + 1) * d]
    vbuf[0, 8 + count : 13 + count] = csum_ref[0:5, :]
    vbuf[0, 13 + count :] = jnp.zeros((vbuf.shape[1] - 13 - count, d), F32)
    def weight(i, _):
        at = pl.ds(pl.multiple_of(i * d, 128), d)
        keep(2 * i, dot_tn(x0_ref[...], dqkv0_ref[:, at]) + dot_tn(x_ref[...], dqkv_ref[:, at]))
        step(after + i, 0)
        return 0

    lax.fori_loop(0, n_in // 2, weight, 0)
    keep(n_in, dot_tn(o0_ref[...], dt0_ref[...]) + dot_tn(o_ref[...], dt_ref[...]))
    begin = after + n_in // 2
    vcopy(0).start()

    def rest(it, _):
        step(it, 0)
        for j in range(4):

            @pl.when(it == begin + LAG * (j + 1))
            def _():
                vcopy(j).wait()
                vbuf[j + 1] = vbuf[j] + vrecv[j]
                if j < 3:
                    vcopy(j + 1).start()

        return 0

    lax.fori_loop(begin, steps + 4 * LAG, rest, 0)
    vsum_ref[...] = vbuf[4]

    @pl.when(second)
    def _():
        for j in range(n_cross):
            over(j).wait_send()


def reduce_scatter(length, dn, saved, w_in, w_out, gain, x0, x1, dqkv0, o0, dt0, parts, encoder, decoder, sums):
    s, d = dn.shape
    rows, width = parts[0].shape[-2:]
    n_in, n_out = dqkv0.shape[1] // width, dt0.shape[1] // width
    counts = (parts[0].shape[0], n_in, n_out, parts[1].shape[0])
    blocks = 2 * counts[0] + sum(counts[1:])
    parts = [part.reshape(part.shape[0], 2, 2, 2, 2, rows, width) for part in parts]
    short = x0.shape[0]
    vec = (24, d)
    vm = pl.BlockSpec(memory_space=pltpu.VMEM)
    sm = pl.BlockSpec(memory_space=pltpu.SMEM)
    shapes = ((s, d), (rows, n_in * width), (rows, n_out * width), (rows, counts[0] * width),
              (counts[0] // 2 * rows, d), (counts[3] // 2 * rows, d), vec)
    return pl.pallas_call(
        functools.partial(reduce_kernel, counts),
        out_shape=(*(jax.ShapeDtypeStruct(shape, F32) for shape in shapes), jax.ShapeDtypeStruct(parts[1].shape, BF)),
        in_specs=[sm] + [vm] * 14 + [pl.BlockSpec(memory_space=pl.ANY)] * 11 + [vm] * 4,
        out_specs=(*(vm,) * 7, pl.BlockSpec(memory_space=pl.ANY)),
        scratch_shapes=[
            pltpu.VMEM((s, 3 * d), BF),
            pltpu.VMEM((s, d), BF),
            pltpu.VMEM((s, d), BF),
            pltpu.VMEM((128, s), F32),
            pltpu.VMEM((8, d), F32),
            pltpu.VMEM((counts[0], 2, 2, 2, 2, rows, width), BF),
            pltpu.VMEM((blocks, 2, 2, 2, rows, width), BF),
            pltpu.VMEM((RING + blocks // 7, 2, 2, 2, rows, width), BF),
            pltpu.VMEM((blocks, 2, 2, rows, width), BF),
            pltpu.VMEM((blocks, 2, rows, width), BF),
            pltpu.VMEM((blocks, rows, width), BF),
            pltpu.VMEM((5, *vec), F32),
            pltpu.VMEM((4, *vec), F32),
            pltpu.VMEM((short, d), F32),
            pltpu.VMEM((s, d), F32),
            pltpu.VMEM((2, short, d), BF),
            pltpu.VMEM((2, s, d), BF),
            pltpu.SemaphoreType.DMA((4, blocks)),
            pltpu.SemaphoreType.DMA((4, blocks)),
            pltpu.SemaphoreType.DMA((blocks,)),
            pltpu.SemaphoreType.DMA((4,)),
            pltpu.SemaphoreType.DMA((4,)),
            pltpu.SemaphoreType.DMA((counts[3],)),
            pltpu.SemaphoreType.DMA((counts[3],)),
            pltpu.SemaphoreType.DMA((3, 2)),
        ],
        compiler_params=pltpu.CompilerParams(collective_id=0, has_side_effects=True, vmem_limit_bytes=67043328),
    )(length.reshape(1, 1), dn, *saved, w_in, w_out, gain, x0, x1, dqkv0, o0, dt0, *parts, *encoder, *decoder, *sums)[:7]


def shards(
    inputs_long,
    inputs_short,
    cotangent_long,
    cotangent_short,
    lengths_long,
    lengths_short,
    self_in_weight,
    self_out_weight,
    expand_weight,
    contract_weight,
    expand_bias,
    layer_biases,
    layer_gains,
    cross_weight,
    cross_biases,
    cross_gain,
):
    decoder = lax.axis_index("section") == 1
    d = inputs_long.shape[-1]
    ff = expand_weight.shape[2]
    w_in, w_out, w_e, w_c = self_in_weight[0], self_out_weight[0], expand_weight[0], contract_weight[0]
    b_e, bias, gain = expand_bias[0], layer_biases[0], layer_gains[0]
    c_gain = cross_gain.reshape(1, d)

    xs = (inputs_short[0, 0], inputs_long[0, 0])
    cots = (cotangent_short[0, 0], cotangent_long[0, 0])
    source = (lengths_short[0, 0], lengths_long[0, 0])
    target = (lengths_short[1, 0], lengths_long[1, 0])
    sizes = tuple(x.shape[0] for x in xs)

    own = tuple(jnp.where(decoder, t, o) for t, o in zip(target, source))

    def attend(i):
        x = xs[i]
        return attn_fwd(x, None, x, w_in, w_out, bias, gain, own[i])

    def encode_ffn(i, n):
        s = sizes[i]

        def decode():
            return blank(((s, d), BF), ((s, ff), BF), ((s, ff), BF), ((s, d), F32), ((s, 128), F32))

        return lax.cond(decoder, decode, lambda: ffn_fwd(n, w_e, w_c, b_e, bias, gain))

    def send(value, steps):
        return lax.ppermute(value, "section", [(0, 1)] if steps > 0 else [(1, 0)])

    def cross(i, memory, n1):
        s = sizes[i]

        def encode():
            return blank(
                ((s, 3 * d), BF), ((s, d), BF), ((s, d), F32), ((s, d), F32), ((s, 128), F32), ((s, d), F32)
            )

        def decode():
            return attn_fwd(n1, memory, n1, cross_weight, None, cross_biases, c_gain, source[i])

        return lax.cond(decoder, decode, encode)

    def turn(i, out):
        s = sizes[i]

        def decode():
            y, g, gp, xhat, r = ffn_fwd(out[5], w_e, w_c, b_e, bias, gain)
            fb = ffn_bwd(cots[i], None, target[i], (gp, xhat, r), w_e, w_c, gain)
            ab = attn_bwd(fb[0], out[:5], cross_weight, None, c_gain, source[i], False)
            return (g, fb[1], fb[2], ab[1], ab[2]), ab[0], ab[3], y, (fb[3], fb[4], ab[4])

        def encode():
            out = blank(
                ((s, ff), BF),
                ((s, ff), BF),
                ((s, d), BF),
                ((s, 3 * d), BF),
                ((s, d), BF),
                ((s, d), F32),
                ((s, d), BF),
                ((s, d), BF),
                ((8, d), F32),
                ((1, ff), F32),
                ((8, d), F32),
            )
            return tuple(out[:5]), out[5], out[6], out[7], tuple(out[8:])

        return lax.cond(decoder, decode, encode)

    att0 = attend(0)
    ffn0 = encode_ffn(0, att0[5])
    mem0 = send(ffn0[0], 1)
    x_long, _ = lax.optimization_barrier((xs[1], ffn0[0]))
    xs = (xs[0], x_long)
    att1 = attend(1)
    n_long, mem0 = lax.optimization_barrier((att1[5], mem0))
    ffn1 = encode_ffn(1, n_long)
    mem1 = send(ffn1[0], 1)
    n_short, _ = lax.optimization_barrier((att0[5], ffn1[0]))
    out0 = cross(0, mem0, n_short)
    keep0, dn0, dm0, y0, sums0 = turn(0, out0)
    back0 = send(dm0, -1)
    n_long, _ = lax.optimization_barrier((att1[5], dm0))
    out1 = cross(1, mem1, n_long)
    n_long, back0 = lax.optimization_barrier((out1[5], back0))
    out1 = (*out1[:5], n_long)
    keep1, dn1, dm1, y1, sums1 = turn(1, out1)
    back1 = send(dm1, -1)
    dp = lax.axis_size("dp")
    staged = dp == 16 and d % (16 * dp) == 0 and d == 6 * 128 and ff == 4 * d

    def cross_grads():
        n1, mem = (att0[5], att1[5]), (mem0, mem1)
        dqkv, dt = ((keep0[j], keep1[j]) for j in (3, 4))
        mixed = (out0[1], out1[1])
        if staged:
            return wgrad_cross(dqkv, dt, n1, mem, mixed, dp)
        joint = jnp.concatenate(dqkv, 0)
        low = jnp.concatenate(n1, 0).astype(BF)
        mem = jnp.concatenate(mem, 0)
        rows = (
            dot_tn(joint[:, :d], low),
            dot_tn(joint[:, d : 2 * d], mem),
            dot_tn(joint[:, 2 * d :], mem),
            dot_tn(jnp.concatenate(dt, 0), jnp.concatenate(mixed, 0)),
        )
        return tuple(jnp.concatenate(rows[j : j + 2], 0).astype(BF) for j in (0, 2))

    def cross_blank():
        shape = (4, dp, d // dp, d // 2) if staged else (2 * d, d)
        return tuple(blank((shape, BF), (shape, BF)))

    cross_sums = sums0[2] + sums1[2]
    cross_first, cross_second = lax.cond(decoder, cross_grads, cross_blank)
    back0, _ = lax.optimization_barrier((back0, cross_first))
    dn0, *enc0 = lax.cond(
        decoder,
        lambda: (dn0, *blank(((sizes[0], ff), BF), ((sizes[0], d), BF), ((8, d), F32), ((1, ff), F32))),
        lambda: tuple(ffn_bwd(cots[0], back0, source[0], ffn0[2:], w_e, w_c, gain)),
    )
    self0 = attn_bwd(dn0, att0[:5], w_in, w_out, gain, own[0], True)
    back1, cross_sent, _ = lax.optimization_barrier((back1, send(cross_sums, -1), self0[0]))
    cross_rows = jnp.where(decoder, cross_sums, cross_sent)

    def plain(left, right):
        left, right = (jnp.concatenate([e.astype(BF) for e in side], 0) for side in (left, right))
        return dot_tn(left, right).astype(BF)

    def contract_grad(g, dt):
        return wgrad_rows(g, dt, dp) if staged else plain(g, dt)

    def decode_last():
        grad = contract_grad((keep0[0], keep1[0]), (keep0[2], keep1[2]))
        return dn1, *blank(((sizes[1], ff), BF)), grad, sums0[0] + sums1[0], sums0[1] + sums1[1]

    def encode_last():
        dn, da, dt, sums, sum_e = ffn_bwd(cots[1], back1, source[1], ffn1[2:], w_e, w_c, gain)
        return dn, da, contract_grad((ffn0[1], ffn1[1]), (enc0[1], dt)), enc0[2] + sums, enc0[3] + sum_e

    dn1, enc_da, g_contract, ffn_sums, sum_e = lax.cond(decoder, decode_last, encode_last)
    if staged:
        dx1, *big, rows = reduce_scatter(
            own[1], dn1, att1[:5], w_in, w_out, gain, xs[0], xs[1], self0[1], att0[1], self0[2],
            (g_contract, cross_first, cross_second),
            (att0[5], att1[5], enc0[0], enc_da),
            (out0[5], out1[5], keep0[1], keep1[1]),
            (self0[4], ffn_sums, sum_e, cross_rows),
        )
    else:
        self1 = attn_bwd(dn1, att1[:5], w_in, w_out, gain, own[1], True)
        dx1 = self1[0]
        self_sums = self0[4] + self1[4]
        rows = [self_sums[0:4], ffn_sums[0:2], self_sums[4:5], ffn_sums[2:3], sum_e.reshape(ff // d, d), cross_rows[0:5]]
        rows = lax.psum(jnp.concatenate(rows, 0), "dp")
        cross_mine = jnp.where(decoder, cross_second, send(cross_first, -1))
        pairs = (((att0[5], enc0[0]), (att1[5], enc_da)), ((out0[5], keep0[1]), (out1[5], keep1[1])))
        g_expand = lax.cond(decoder, lambda: plain(*zip(*pairs[1])), lambda: plain(*zip(*pairs[0])))
        in_grad = plain(xs, (self0[1], self1[1]))
        out_grad = plain((att0[1], att1[1]), (self0[2], self1[2]))
        big = [
            lax.psum_scatter(part, "dp", scatter_dimension=0, tiled=True).astype(F32)
            for part in (in_grad, out_grad, g_expand, g_contract, cross_mine)
        ]
    count = 8 + ff // d
    me = lax.axis_index("dp")
    piece = lax.dynamic_slice_in_dim(rows[:8], me * (d // dp), d // dp, 1)
    e_piece = lax.dynamic_slice_in_dim(rows[8:count].reshape(1, ff), me * (ff // dp), ff // dp, 1)
    outs = [jnp.where(decoder, y, e)[None, None] for y, e in ((y0, ffn0[0]), (y1, ffn1[0]))]
    return (
        outs[1],
        outs[0],
        dx1[None, None],
        self0[0][None, None],
        big[0][None],
        big[1][None],
        big[2][None],
        big[3][None],
        e_piece,
        piece[None, :6],
        piece[None, 6:8],
        big[4].T,
        rows[count : count + 4],
        rows[count + 4],
    )


def solution(mesh):
    in_specs = (
        P("section", "dp", None, None),
        P("section", "dp", None, None),
        P("section", "dp", None, None),
        P("section", "dp", None, None),
        P(None, "dp"),
        P(None, "dp"),
        P("section", None, None),
        P("section", None, None),
        P("section", None, None),
        P("section", None, None),
        P("section", None),
        P("section", None, None),
        P("section", None, None),
        P(),
        P(),
        P(),
    )
    out_specs = (
        P("section", "dp", None, None),
        P("section", "dp", None, None),
        P("section", "dp", None, None),
        P("section", "dp", None, None),
        P("section", "dp", None),
        P("section", "dp", None),
        P("section", "dp", None),
        P("section", "dp", None),
        P("section", "dp"),
        P("section", None, "dp"),
        P("section", None, "dp"),
        P(None, ("section", "dp")),
        P(),
        P(),
    )
    return jax.shard_map(shards, mesh=mesh, in_specs=in_specs, out_specs=out_specs, check_vma=False)
```

profile of v0, /device:TPU:0, one launch (start us, length us, event | category | flops | bytes accessed | tf_op | source)
XLA Modules:
  0.0 358.4 jit_solution(15518553767099783288)
XLA Ops:
  3.9 9.8 %shard_map.263 = (bf16[256,2304]{1,0:T(8,128)(2,1)}, bf16[256,768]{1,0:T(8,128)(2,1)}, f32[256,768]{1,0:T(8,128)}, f32[256,768]{1,0:T(8,128)}, f32[256,128]{1,0:T(8,128)}, /*index=5*/f32[256,768]{1,0:T(8,128)S(1)}) custom-call(s32[1,1]{1,0:T(1,128)} %bitcast.12.len_ref.refs_0_, bf16[256,768]{1,0:T(8,128)(2,1)} %bitcast.77, bf16[256,768]{1,0:T(8,128)(2,1)} %bitcast.78, ...), custom_call_target="tpu_custom_call" | custom-call | tf_op jit(solution)/shard_map/pallas_call | solution.py:110
  13.7 9.8 %conditional.9 = ((bf16[256,768]{1,0:T(8,128)(2,1)}, bf16[256,3072]{1,0:T(8,128)(2,1)}, bf16[256,3072]{1,0:T(8,128)(2,1)}, f32[256,768]{1,0:T(8,128)}, f32[256,128]{1,0:T(8,128)})) conditional(s32[]{:T(128)} %convert_element_type.2, (f32[256,768]{1,0:T(8,128)S(1)}, bf16[768,3072]{1,0:T(8,128)(2,1)}, bf16[3072,768]{1,0:T(8,128)(2,1)}, ...), branch_computations={%region_0.1_spmd, %region_1.2_spmd} | conditional | bytes 8 | solution.py:769
  13.7 9.8 %branch_0_fun.11 = (bf16[256,768]{1,0:T(8,128)(2,1)}, bf16[256,3072]{1,0:T(8,128)(2,1)}, bf16[256,3072]{1,0:T(8,128)(2,1)}, f32[256,768]{1,0:T(8,128)}, f32[256,128]{1,0:T(8,128)}) custom-call(f32[256,768]{1,0:T(8,128)S(1)} %get-tuple-element.224.n_ref, bf16[768,3072]{1,0:T(8,128)(2,1)} %get-tuple-element.225.we_ref, ...), custom_call_target="tpu_custom_call" | custom-call | tf_op jit(solution)/shard_map/cond/branch_0_fun/pallas_call | solution.py:251
  26.7 20.2 %shard_map.264 = (bf16[640,2304]{1,0:T(8,128)(2,1)}, bf16[640,768]{1,0:T(8,128)(2,1)}, f32[640,768]{1,0:T(8,128)}, f32[640,768]{1,0:T(8,128)}, f32[640,128]{1,0:T(8,128)}, /*index=5*/f32[640,768]{1,0:T(8,128)S(1)}) custom-call(s32[1,1]{1,0:T(1,128)} %bitcast.8.len_ref.refs_0_, bf16[640,768]{1,0:T(8,128)(2,1)} %bitcast.73, bf16[640,768]{1,0:T(8,128)(2,1)} %bitcast.74, ...), custom_call_target="tpu_custom_call" | custom-call | tf_op jit(solution)/shard_map/pallas_call | solution.py:110
  47.8 17.4 %conditional.10 = ((bf16[640,768]{1,0:T(8,128)(2,1)}, bf16[640,3072]{1,0:T(8,128)(2,1)}, bf16[640,3072]{1,0:T(8,128)(2,1)}, f32[640,768]{1,0:T(8,128)}, f32[640,128]{1,0:T(8,128)})) conditional(s32[]{:T(128)} %convert_element_type.2, (f32[640,768]{1,0:T(8,128)S(1)}, bf16[768,3072]{1,0:T(8,128)(2,1)}, bf16[3072,768]{1,0:T(8,128)(2,1)}, ...), branch_computations={%region_2.3_spmd, %region_3.4_spmd} | conditional | bytes 8 | solution.py:769
  48.0 17.2 %branch_0_fun.12 = (bf16[640,768]{1,0:T(8,128)(2,1)}, bf16[640,3072]{1,0:T(8,128)(2,1)}, bf16[640,3072]{1,0:T(8,128)(2,1)}, f32[640,768]{1,0:T(8,128)}, f32[640,128]{1,0:T(8,128)}) custom-call(f32[640,768]{1,0:T(8,128)S(1)} %get-tuple-element.230.n_ref, bf16[768,3072]{1,0:T(8,128)(2,1)} %get-tuple-element.231.we_ref, ...), custom_call_target="tpu_custom_call" | custom-call | tf_op jit(solution)/shard_map/cond/branch_0_fun/pallas_call | solution.py:251
  65.2 2.3 collective-permute-start.1
  69.7 19.0 %collective-permute-done.1 = bf16[640,768]{1,0:T(8,128)(2,1)} collective-permute-done((bf16[640,768]{1,0:T(8,128)(2,1)}, bf16[640,768]{1,0:T(8,128)(2,1)}, u32[]{:S(2)}, u32[]{:S(2)}) %collective-permute-start.1) | collective-permute-done | bytes 983072 | tf_op jit(solution)/shard_map/ppermute | solution.py:772
  88.7 12.1 %conditional.13 = ((bf16[640,2304]{1,0:T(8,128)(2,1)}, bf16[640,768]{1,0:T(8,128)(2,1)}, f32[640,768]{1,0:T(8,128)}, f32[640,768]{1,0:T(8,128)}, f32[640,128]{1,0:T(8,128)}, /*index=5*/f32[640,768]{1,0:T(8,128)})) conditional(s32[]{:T(128)} %convert_element_type.2, () %tuple.92, (s32[1,1]{1,0:T(1,128)}, f32[640,768]{1,0:T(8,128)S(1)}, ...), branch_computations={%region_8.9_spmd, %region_9.10_spmd} | conditional | bytes 8 | solution.py:785
  100.8 6.9 %conditional.14 = ((bf16[640,3072]{1,0:T(8,128)(2,1)}, bf16[640,3072]{1,0:T(8,128)(2,1)}, bf16[640,768]{1,0:T(8,128)(2,1)}, bf16[640,2304]{1,0:T(8,128)(2,1)}, b...) conditional(s32[]{:T(128)} %convert_element_type.2, () %tuple.91, ...), branch_computations={%region_10.11_spmd, %region_11.12_spmd} | conditional | bytes 1335420 | solution.py:812
  109.1 1.8 select_bitcast_fusion.1
  110.9 1.4 add.21
  113.6 2.3 select_bitcast_fusion
  115.9 9.5 %conditional.15 = ((f32[256,768]{1,0:T(8,128)}, bf16[256,3072]{1,0:T(8,128)(2,1)}, bf16[256,768]{1,0:T(8,128)(2,1)}, f32[8,768]{1,0:T(8,128)}, f32[1,3072]{1,0:T(1,128)})) conditional(s32[]{:T(128)} %convert_element_type.2, (s32[1,1]{1,0:T(1,128)}, bf16[256,768]{1,0:T(8,128)(2,1)S(1)}, bf16[256,768]{1,0:T(8,128)(2,1)}, ...), branch_computations={%region_12.13_spmd, %region_13.14_spmd} | conditional | bytes 48 | solution.py:860
  115.9 9.5 %branch_0_fun.17 = (f32[256,768]{1,0:T(8,128)}, bf16[256,3072]{1,0:T(8,128)(2,1)}, bf16[256,768]{1,0:T(8,128)(2,1)}, f32[8,768]{1,0:T(8,128)}, f32[1,3072]{1,0:T(1,128)}) custom-call(s32[1,1]{1,0:T(1,128)} %get-tuple-element.321.len_ref, bf16[256,768]{1,0:T(8,128)(2,1)S(1)} %get-tuple-element.322.cot_ref, bf16[256,768]{1,0:T(8,128)(2,1)} %get-tuple-element.323.dm_ref, ...), custom_call_target="tpu_custom_call" | custom-call | tf_op jit(solution)/shard_map/cond/branch_0_fun/pallas_call | solution.py:301
  125.5 11.3 %shard_map.265 = (f32[256,768]{1,0:T(8,128)}, bf16[256,2304]{1,0:T(8,128)(2,1)}, bf16[256,768]{1,0:T(8,128)(2,1)}, bf16[8,128]{1,0:T(8,128)(2,1)}, f32[8,768]{1,0:T(8,128)}) custom-call(s32[1,1]{1,0:T(1,128)} %bitcast.12.len_ref.refs_0_, f32[256,768]{1,0:T(8,128)} %get-tuple-element.511.refs_1_, bf16[256,2304]{1,0:T(8,128)(2,1)} %get-tuple-element.512.refs_2_, ...), custom_call_target="tpu_custom_call" | custom-call | tf_op jit(solution)/shard_map/pallas_call | solution.py:205
  136.8 70.6 %collective-permute-done.4 = f32[8,768]{1,0:T(8,128)} collective-permute-done((f32[8,768]{1,0:T(8,128)}, f32[8,768]{1,0:T(8,128)}, u32[]{:S(2)}, u32[]{:S(2)}) %collective-permute-start.4) | collective-permute-done | bytes 24608 | tf_op jit(solution)/shard_map/ppermute | solution.py:772
  207.4 1.4 broadcast_select_fusion.refs_29_
  208.8 24.0 %conditional.16 = (f32[640,768]{1,0:T(8,128)}, bf16[640,3072]{1,0:T(8,128)(2,1)}, f32[8,768]{1,0:T(8,128)}, f32[1,3072]{1,0:T(1,128)}, bf16[8,2,2,2,2,48,384]{6,5,4,3,2,1,0:T(8,128)(2,1)}) conditional(s32[]{:T(128)} %convert_element_type.2, (s32[1,1]{1,0:T(1,128)}, bf16[640,768]{1,0:T(8,128)(2,1)S(1)}, bf16[640,768]{1,0:T(8,128)(2,1)}, ...), branch_computations={%region_14.15_spmd, %region_15.16_spmd} | conditional | flops 9216 | bytes 10334304 | solution.py:884
  209.0 13.6 %branch_0_fun.18 = (f32[640,768]{1,0:T(8,128)}, bf16[640,3072]{1,0:T(8,128)(2,1)}, bf16[640,768]{1,0:T(8,128)(2,1)}, f32[8,768]{1,0:T(8,128)}, f32[1,3072]{1,0:T(1,128)}) custom-call(s32[1,1]{1,0:T(1,128)} %get-tuple-element.334.len_ref, bf16[640,768]{1,0:T(8,128)(2,1)S(1)} %get-tuple-element.335.cot_ref, bf16[640,768]{1,0:T(8,128)(2,1)} %get-tuple-element.336.dm_ref, ...), custom_call_target="tpu_custom_call" | custom-call | tf_op jit(solution)/shard_map/cond/branch_0_fun/pallas_call | solution.py:301
  222.6 9.0 %branch_0_fun.19 = bf16[8,16,48,384]{3,2,1,0:T(8,128)(2,1)} custom-call(bf16[256,3072]{1,0:T(8,128)(2,1)} %get-tuple-element.349.refs_0_, bf16[640,3072]{1,0:T(8,128)(2,1)} %get-tuple-element.350.refs_1_, bf16[256,768]{1,0:T(8,128)(2,1)S(1)} %get-tuple-element.351.refs_2_, bf16[640,768]{1,0:T(8,128)(2,1)} %get-tuple-element.352.refs_3_), custom_call_target="tpu_custom_call" | custom-call | tf_op jit(solution)/shard_map/cond/branch_0_fun/pallas_call | solution.py:347
  232.8 113.1 %shard_map.266 = (f32[640,768]{1,0:T(8,128)}, f32[48,2304]{1,0:T(8,128)}, f32[48,768]{1,0:T(8,128)}, f32[48,3072]{1,0:T(8,128)}, f32[192,768]{1,0:T(8,128)}, /*i...) custom-call(s32[1,1]{1,0:T(1,128)} %bitcast.8.len_ref.refs_0_, ...), custom_call_target="tpu_custom_call" | custom-call | tf_op jit(solution)/shard_map/pallas_call | solution.py:690
  348.0 1.4 fusion
  351.3 3.0 copy.161
  (88 shorter events, 18.6 us)
Async XLA Ops:
  2.7 44.3 %copy-start.7 = (f32[1,6,768]{2,1,0:T(8,128)}, f32[1,6,768]{2,1,0:T(8,128)S(1)}, u32[]{:S(2)}) copy-start(f32[1,6,768]{2,1,0:T(8,128)S(1)} %copy.42) | copy-start | bytes 55300
  3.9 9.8 %copy-start.9 = (f32[1,2,768]{2,1,0:T(2,128)S(1)}, f32[1,2,768]{2,1,0:T(2,128)}, u32[]{:S(2)}) copy-start(f32[1,2,768]{2,1,0:T(2,128)} %param.46) | copy-start | bytes 18436
  3.9 9.8 %copy-start.17 = (f32[1,3072]{1,0:T(1,128)S(1)}, f32[1,3072]{1,0:T(1,128)}, u32[]{:S(2)}) copy-start(f32[1,3072]{1,0:T(1,128)} %param.44) | copy-start | bytes 36868
  13.7 111.6 %copy-start.1 = (f32[256,768]{1,0:T(8,128)}, f32[256,768]{1,0:T(8,128)S(1)}, u32[]{:S(2)}) copy-start(f32[256,768]{1,0:T(8,128)S(1)} %get-tuple-element.484.refs_18_) | copy-start | bytes 2359300
  13.7 11.1 %copy-start.30 = (s32[2,1]{0,1:T(1,128)S(1)}, s32[2,1]{0,1:T(1,128)}, u32[]{:S(2)}) copy-start(s32[2,1]{0,1:T(1,128)} %param.38) | copy-start | bytes 28
  23.5 23.5 %collective-permute-start = (bf16[256,768]{1,0:T(8,128)(2,1)}, bf16[256,768]{1,0:T(8,128)(2,1)S(1)}, u32[]{:S(2)}, u32[]{:S(2)}) collective-permute-start(bf16[256,768]{1,0:T(8,128)(2,1)} %get-tuple-element.479), channel_id=1, source_target_pairs={{0,16},{1,17},{2,18},{3,19},{4,20},{5,21},{6,22},{7,23},{8,24},{9,... | collective-permute-start | bytes 1179656 | tf_op jit(solution)/shard_map/ppermute | solution.py:772
  47.0 78.3 %copy-start = (f32[640,768]{1,0:T(8,128)}, f32[640,768]{1,0:T(8,128)S(1)}, u32[]{:S(2)}) copy-start(f32[640,768]{1,0:T(8,128)S(1)} %get-tuple-element.493.refs_19_) | copy-start | bytes 5898244
  47.0 20.4 %copy-start.29 = (f32[768]{0:T(1024)S(1)}, f32[768]{0:T(1024)}, u32[]{:S(2)}) copy-start(f32[768]{0:T(1024)} %param.49) | copy-start | bytes 9220
  65.2 23.5 %collective-permute-start.1 = (bf16[640,768]{1,0:T(8,128)(2,1)}, bf16[640,768]{1,0:T(8,128)(2,1)}, u32[]{:S(2)}, u32[]{:S(2)}) collective-permute-start(bf16[640,768]{1,0:T(8,128)(2,1)} %get-tuple-element.483), channel_id=1, source_target_pairs={{0,16},{1,17},{2,18},{3,19},{4,20},{5,21},{6,22},{7,23},{8,24},{9,... | collective-permute-start | bytes 2949128 | tf_op jit(solution)/shard_map/ppermute | solution.py:772
  68.4 32.4 %collective-permute-start.2 = (bf16[256,768]{1,0:T(8,128)(2,1)}, bf16[256,768]{1,0:T(8,128)(2,1)}, u32[]{:S(2)}, u32[]{:S(2)}) collective-permute-start(bf16[256,768]{1,0:T(8,128)(2,1)} %get-tuple-element.492), channel_id=1, source_target_pairs={{16,0},{17,1},{18,2},{19,3},{20,4},{21,5},{22,6},{23,7},{24,8},{25... | collective-permute-start | bytes 1179656 | tf_op jit(solution)/shard_map/ppermute | solution.py:772
  107.8 99.6 %collective-permute-start.3 = (bf16[640,768]{1,0:T(8,128)(2,1)}, bf16[640,768]{1,0:T(8,128)(2,1)}, u32[]{:S(2)}, u32[]{:S(2)}) collective-permute-start(bf16[640,768]{1,0:T(8,128)(2,1)} %get-tuple-element.503), channel_id=1, source_target_pairs={{16,0},{17,1},{18,2},{19,3},{20,4},{21,5},{22,6},{23,7},{24,8},{25... | collective-permute-start | bytes 2949128 | tf_op jit(solution)/shard_map/ppermute | solution.py:772
  112.3 95.1 %collective-permute-start.4 = (f32[8,768]{1,0:T(8,128)}, f32[8,768]{1,0:T(8,128)}, u32[]{:S(2)}, u32[]{:S(2)}) collective-permute-start(f32[8,768]{1,0:T(8,128)} %add.21), channel_id=1, source_target_pairs={{16,0},{17,1},{18,2},{19,3},{20,4},{21,5},{22,6},{23,7},{24,8},{25... | collective-permute-start | bytes 73736 | tf_op jit(solution)/shard_map/ppermute | solution.py:772
  125.4 83.4 %copy-start.2 = (bf16[1,1,640,768]{3,2,1,0:T(8,128)(2,1)S(1)}, bf16[1,1,640,768]{3,2,1,0:T(8,128)(2,1)}, u32[]{:S(2)}) copy-start(bf16[1,1,640,768]{3,2,1,0:T(8,128)(2,1)} %param.36) | copy-start | bytes 2949124
  125.4 83.4 %copy-start.3 = (f32[640,768]{1,0:T(8,128)S(1)}, f32[640,768]{1,0:T(8,128)}, u32[]{:S(2)}) copy-start(f32[640,768]{1,0:T(8,128)} %get-tuple-element.520) | copy-start | bytes 5898244
  125.4 83.3 %copy-start.13 = (bf16[256,768]{1,0:T(8,128)(2,1)S(1)}, bf16[256,768]{1,0:T(8,128)(2,1)}, u32[]{:S(2)}) copy-start(bf16[256,768]{1,0:T(8,128)(2,1)} %get-tuple-element.533) | copy-start | bytes 1179652
  125.4 83.3 %copy-start.14 = (bf16[256,768]{1,0:T(8,128)(2,1)S(1)}, bf16[256,768]{1,0:T(8,128)(2,1)}, u32[]{:S(2)}) copy-start(bf16[256,768]{1,0:T(8,128)(2,1)} %get-tuple-element.526) | copy-start | bytes 1179652
  125.4 83.3 %copy-start.21 = (f32[8,768]{1,0:T(8,128)S(1)}, f32[8,768]{1,0:T(8,128)}, u32[]{:S(2)}) copy-start(f32[8,768]{1,0:T(8,128)} %get-tuple-element.527) | copy-start | bytes 73732
  125.4 83.3 %copy-start.22 = (f32[8,768]{1,0:T(8,128)S(1)}, f32[8,768]{1,0:T(8,128)}, u32[]{:S(2)}) copy-start(f32[8,768]{1,0:T(8,128)} %get-tuple-element.528) | copy-start | bytes 73732
  125.4 83.3 %copy-start.24 = (f32[8,768]{1,0:T(8,128)S(1)}, f32[8,768]{1,0:T(8,128)}, u32[]{:S(2)}) copy-start(f32[8,768]{1,0:T(8,128)} %get-tuple-element.522) | copy-start | bytes 73732
  125.4 83.3 %copy-start.25 = (f32[1,3072]{1,0:T(1,128)S(1)}, f32[1,3072]{1,0:T(1,128)}, u32[]{:S(2)}) copy-start(f32[1,3072]{1,0:T(1,128)} %get-tuple-element.529) | copy-start | bytes 36868
  125.5 83.3 %copy-start.26 = (f32[1,3072]{1,0:T(1,128)S(1)}, f32[1,3072]{1,0:T(1,128)}, u32[]{:S(2)}) copy-start(f32[1,3072]{1,0:T(1,128)} %get-tuple-element.530) | copy-start | bytes 36868
  125.5 83.3 %copy-start.28 = (f32[1,3072]{1,0:T(1,128)S(1)}, f32[1,3072]{1,0:T(1,128)}, u32[]{:S(2)}) copy-start(f32[1,3072]{1,0:T(1,128)} %get-tuple-element.523) | copy-start | bytes 36868
  222.6 9.0 %copy-start.27 = (f32[1,3072]{1,0:T(1,128)S(1)}, f32[1,3072]{1,0:T(1,128)}, u32[]{:S(2)}) copy-start(f32[1,3072]{1,0:T(1,128)} %get-tuple-element.348) | copy-start | bytes 36868 | tf_op jit(solution)/shard_map/cond
  222.6 9.6 %copy-start.23 = (f32[8,768]{1,0:T(8,128)S(1)}, f32[8,768]{1,0:T(8,128)}, u32[]{:S(2)}) copy-start(f32[8,768]{1,0:T(8,128)} %get-tuple-element.346) | copy-start | bytes 73732 | tf_op jit(solution)/shard_map/cond
  (8 other events, 25.2 us)
where the time goes:
time: 360 us; the launch traced here: 358 us
  Pallas kernels  213 us (59%)
  waiting for transfers between devices  89.6 us (25%)
  loops' own time  19.5 us (5%)
  local copies, waits for them, and re-layouts  16.6 us (5%)
  other arithmetic  8.06 us (2%)
  starting transfers between devices  7.42 us (2%)
  between operations  3.73 us (1%)
    pallas_call x1, Pallas kernels, reduce_scatter(): pl.pallas_call(functools.partial(reduce_kernel, counts), out_shape=(*(jax...  113 us
    ppermute x5, waiting for transfers between devices, send(): return lax.ppermute(value, 'section', [(0, 1)] if steps > 0 else [(1, 0)])  89.6 us
    pallas_call x2, Pallas kernels, attn_fwd(): pl.pallas_call(functools.partial(attn_fwd_kernel, same), out_shape=(jax.S...  30.1 us
    pallas_call x2, Pallas kernels, ffn_fwd(): pl.pallas_call(ffn_fwd_kernel, out_shape=(jax.ShapeDtypeStruct((s, d), BF...  26.9 us
    pallas_call x2, Pallas kernels, ffn_bwd(): pl.pallas_call(functools.partial(ffn_bwd_kernel, extra), out_shape=(jax.S...  23.1 us
    another operation x2, loops' own time, cross(): return lax.cond(decoder, decode, encode)  12.1 us
    pallas_call x1, Pallas kernels, attn_bwd(): pl.pallas_call(functools.partial(attn_bwd_kernel, same), out_shape=(jax.S...  11.3 us
    unnamed x59, local copies, waits for them, and re-layouts  9.95 us
  transfers between devices with their start and end apart: 5, of which 2 were waited for; matrix products, arithmetic and copies ran while one was open for 2% of the time, Pallas kernels for 11%

commit v1 on v0

--- a/solution.py
+++ b/solution.py
@@ -119,11 +119,9 @@
     h = dn * gain
     return r * (h - jnp.mean(h, axis=-1, keepdims=True) - xhat * jnp.mean(h * xhat, axis=-1, keepdims=True))
 
-def attn_bwd_body(same, between, len_ref, dn_ref, qkv_ref, o_ref, lse_ref, xhat_ref, r_ref, wqkv_ref, wo_ref, gain_ref,
+def attn_bwd_body(same, between, ready, len_ref, dn_ref, qkv_ref, o_ref, lse_ref, xhat_ref, r_ref, wqkv_ref, wo_ref, gain_ref,
                   dres_ref, dqkv_ref, dt_ref, dkvx_ref, sums_ref, do_ref, dq_ref):
     s, d = dn_ref.shape
-    if not same:
-        wo_ref = wqkv_ref.at[:, 3 * d :]
     dn = dn_ref[...]
     xhat = xhat_ref[...]
     du = norm_backward(dn, xhat, r_ref[:, :1], gain_ref[0:1, :])
@@ -133,6 +131,7 @@
     sums_ref[3:4, :] = jnp.sum(dn, axis=0, keepdims=True)
     sums_ref[4:5, :] = jnp.sum(dn * xhat, axis=0, keepdims=True)
     dres_ref[...] = du
+    ready(2)
     do_ref[...] = dot_nt(dt, wo_ref[...]).astype(BF)
     length = len_ref[0, 0]
     lane = lanes(s)
@@ -181,7 +180,9 @@
         dqkv_ref[:, pl.ds(d + at, 128)] = jnp.where(m1, dk[0], dk[1]).astype(BF)
         dqkv_ref[:, pl.ds(2 * d + at, 128)] = jnp.where(m1, dv[0], dv[1]).astype(BF)
         return 0
+    ready(0)
     lax.fori_loop(0, d // 128, pair, 0)
+    ready(1)
     if same:
         dres_ref[...] += dot_nt(dqkv_ref[...], wqkv_ref[...])
     else:
@@ -191,25 +192,47 @@
     sums_ref[1:2, :] = jnp.sum(dqkv_ref[:, 2*d:].astype(F32), axis=0, keepdims=True)
     sums_ref[5:8, :] = jnp.zeros((3, d), F32)
 
-def attn_bwd_kernel(same, *refs):
-    attn_bwd_body(same, lambda p: None, *refs)
+def incoming(sources, targets, sems):
+    return [pltpu.make_async_copy(src, dst, sems.at[k]) for k, (src, dst) in enumerate(zip(sources, targets))]
+
+
+def attn_bwd_kernel(len_ref, dn_ref, qkv_hbm, o_hbm, lse_hbm, xhat_ref, r_ref, w_hbm, wo_hbm, gain_ref,
+                    dres_ref, dqkv_ref, dt_ref, dkvx_ref, sums_ref, do_ref, dq_ref, qkv_ref, o_ref, lse_ref, w_ref, wo_ref, sems):
+    d = dn_ref.shape[1]
+    same = wo_hbm.shape[1] == d
+    copies = incoming(
+        (wo_hbm.at[:, wo_hbm.shape[1] - d :], qkv_hbm, o_hbm, lse_hbm, w_hbm.at[:, : 3 * d]),
+        (wo_ref, qkv_ref, o_ref, lse_ref, w_ref),
+        sems,
+    )
+    for copy in copies:
+        copy.start()
+
+    def ready(stage):
+        for copy in (copies[1:4], copies[4:], copies[:1])[stage]:
+            copy.wait()
+
+    attn_bwd_body(same, lambda p: None, ready, len_ref, dn_ref, qkv_ref, o_ref, lse_ref, xhat_ref, r_ref, w_ref, wo_ref,
+                  gain_ref, dres_ref, dqkv_ref, dt_ref, dkvx_ref, sums_ref, do_ref, dq_ref)
 
 
 def attn_bwd(dn, saved, wqkv, wo, gain, length, same):
     qkv, o, lse, xhat, r = saved
     s, d = dn.shape
-    if not same:
-        wo = gain
     vm = pl.BlockSpec(memory_space=pltpu.VMEM)
     sm = pl.BlockSpec(memory_space=pltpu.SMEM)
+    hbm = pl.BlockSpec(memory_space=pl.ANY)
     return pl.pallas_call(
-        functools.partial(attn_bwd_kernel, same),
+        attn_bwd_kernel,
         out_shape=(jax.ShapeDtypeStruct((s, d), F32), jax.ShapeDtypeStruct((s, 3 * d), BF), jax.ShapeDtypeStruct((s, d), BF),
                    jax.ShapeDtypeStruct((8, 128) if same else (s, d), BF), jax.ShapeDtypeStruct((8, d), F32)),
-        in_specs=[sm] + [vm] * 9, out_specs=(vm,) * 5,
-        scratch_shapes=[pltpu.VMEM((s, d), BF), pltpu.VMEM((128, s), F32)],
+        in_specs=[sm, vm, hbm, hbm, hbm, vm, vm, hbm, hbm, vm], out_specs=(vm,) * 5,
+        scratch_shapes=[pltpu.VMEM((s, d), BF), pltpu.VMEM((128, s), F32), pltpu.VMEM((s, 3 * d), BF),
+                        pltpu.VMEM((s, d), BF), pltpu.VMEM((s, d), F32), pltpu.VMEM((d, 3 * d), BF),
+                        pltpu.VMEM((d, d), BF), pltpu.SemaphoreType.DMA((5,))],
         compiler_params=pltpu.CompilerParams(vmem_limit_bytes=60 << 20),
-    )(length.reshape(1, 1), dn, qkv, o, lse, xhat, r, wqkv, wo, gain)
+    )(length.reshape(1, 1), dn, qkv, o, lse, xhat, r, wqkv, wo if same else wqkv, gain)
+
 
 def gelu_parts(a):
     e = jnp.exp(-0.5 * a * a)
@@ -297,7 +320,7 @@
     columns = pl.BlockSpec((s, chunk), lambda c: (0, c))
     row = pl.BlockSpec((1, chunk), lambda c: (0, c))
     if not extra:
-        dm = cot[:8]
+        dm = gain
     return pl.pallas_call(
         functools.partial(ffn_bwd_kernel, extra),
         out_shape=(jax.ShapeDtypeStruct((s, d), F32), jax.ShapeDtypeStruct((s, ff), BF), jax.ShapeDtypeStruct((s, d), BF),
@@ -391,14 +414,19 @@
 
 
 def reduce_kernel(counts, *refs):
-    (len_ref, dn_ref, qkv_ref, o_ref, lse_ref, xhat_ref, r_ref, wqkv_ref, wo_ref, gain_ref) = refs[:10]
-    (x0_ref, x_ref, dqkv0_ref, o0_ref, dt0_ref, contract, cross_first, cross_second) = refs[10:18]
+    (len_ref, dn_ref, qkv_hbm, o_hbm, lse_hbm, xhat_ref, r_ref, w_hbm, wo_ref, gain_ref) = refs[:10]
+    (contract, cross_first, cross_second) = refs[15:18]
     ffn_refs = (refs[18:22], refs[22:26])
     (ssum_ref, fsum_ref, esum_ref, csum_ref) = refs[26:30]
     (dres_ref, in_ref, out_ref, expand_ref, contract_ref, cross_ref, vsum_ref, landed) = refs[30:38]
     (dqkv_ref, dt_ref, do_ref, dq_ref, sums_ref, made, own, r0, r1, r2, r3, vbuf, vrecv) = refs[38:51]
     (n0_buf, n1_buf, da0_buf, da1_buf) = refs[51:55]
-    send_sem, recv_sem, local_sem, vsend_sem, vrecv_sem, xsend_sem, xrecv_sem, fetch_sem = refs[55:]
+    held = refs[55:64]
+    (qkv_ref, o_ref, lse_ref, wqkv_ref, x0_ref, x_ref, dqkv0_ref, o0_ref, dt0_ref) = held
+    send_sem, recv_sem, local_sem, vsend_sem, vrecv_sem, xsend_sem, xrecv_sem, fetch_sem, held_sem = refs[64:]
+    copies = incoming((qkv_hbm, o_hbm, lse_hbm, w_hbm, *refs[10:15]), held, held_sem)
+    for copy in copies[:3]:
+        copy.start()
     d = dn_ref.shape[1]
     n_ffn, n_in, n_out, n_cross = 2 * counts[0], counts[1], counts[2], counts[3]
     blocks = n_ffn + n_in + n_out + n_cross
@@ -439,6 +467,8 @@
             copy.start()
 
     chosen(begin_fetch)
+    for copy in copies[3:]:
+        copy.start()
     pl.semaphore_wait(barrier, 5)
 
     def over(j):
@@ -625,9 +655,13 @@
 
         some(jnp.minimum(3 + 2 * p, 7 + p), jnp.minimum(5 + 2 * p, 8 + p))
 
+    def ready(stage):
+        for copy in (copies[:3], copies[3:], ())[stage]:
+            copy.wait()
+
     some(0, 3)
     attn_bwd_body(
-        True, beside,
+        True, beside, ready,
         len_ref, dn_ref, qkv_ref, o_ref, lse_ref, xhat_ref, r_ref, wqkv_ref, wo_ref, gain_ref,
         dres_ref, dqkv_ref, dt_ref, None, sums_ref, do_ref, dq_ref,
     )
@@ -685,13 +719,14 @@
     vec = (24, d)
     vm = pl.BlockSpec(memory_space=pltpu.VMEM)
     sm = pl.BlockSpec(memory_space=pltpu.SMEM)
+    hbm = pl.BlockSpec(memory_space=pl.ANY)
     shapes = ((s, d), (rows, n_in * width), (rows, n_out * width), (rows, counts[0] * width),
               (counts[0] // 2 * rows, d), (counts[3] // 2 * rows, d), vec)
     return pl.pallas_call(
         functools.partial(reduce_kernel, counts),
         out_shape=(*(jax.ShapeDtypeStruct(shape, F32) for shape in shapes), jax.ShapeDtypeStruct(parts[1].shape, BF)),
-        in_specs=[sm] + [vm] * 14 + [pl.BlockSpec(memory_space=pl.ANY)] * 11 + [vm] * 4,
-        out_specs=(*(vm,) * 7, pl.BlockSpec(memory_space=pl.ANY)),
+        in_specs=[sm, vm, hbm, hbm, hbm, vm, vm, hbm, vm, vm] + [hbm] * 16 + [vm] * 4,
+        out_specs=(*(vm,) * 7, hbm),
         scratch_shapes=[
             pltpu.VMEM((s, 3 * d), BF),
             pltpu.VMEM((s, d), BF),
@@ -710,6 +745,15 @@
             pltpu.VMEM((s, d), F32),
             pltpu.VMEM((2, short, d), BF),
             pltpu.VMEM((2, s, d), BF),
+            pltpu.VMEM((s, 3 * d), BF),
+            pltpu.VMEM((s, d), BF),
+            pltpu.VMEM((s, d), F32),
+            pltpu.VMEM((d, 3 * d), BF),
+            pltpu.VMEM((short, d), BF),
+            pltpu.VMEM((s, d), BF),
+            pltpu.VMEM((short, 3 * d), BF),
+            pltpu.VMEM((short, d), BF),
+            pltpu.VMEM((short, d), BF),
             pltpu.SemaphoreType.DMA((4, blocks)),
             pltpu.SemaphoreType.DMA((4, blocks)),
             pltpu.SemaphoreType.DMA((blocks,)),
@@ -718,6 +762,7 @@
             pltpu.SemaphoreType.DMA((counts[3],)),
             pltpu.SemaphoreType.DMA((counts[3],)),
             pltpu.SemaphoreType.DMA((3, 2)),
+            pltpu.SemaphoreType.DMA((9,)),
         ],
         compiler_params=pltpu.CompilerParams(collective_id=0, has_side_effects=True, vmem_limit_bytes=67043328),
     )(length.reshape(1, 1), dn, *saved, w_in, w_out, gain, x0, x1, dqkv0, o0, dt0, *parts, *encoder, *decoder, *sums)[:7]

time: 360 us -> 355 us (0.986)
    unnamed x59 -> x53, local copies, waits for them, and re-layouts: 9.95 us -> 9.94 us
where the time goes in v1:
time: 355 us; the launch traced here: 353 us
  Pallas kernels  211 us (59%)
  waiting for transfers between devices  87 us (25%)
  loops' own time  19.6 us (6%)
  local copies, waits for them, and re-layouts  16.6 us (5%)
  other arithmetic  8.03 us (2%)
  starting transfers between devices  7.4 us (2%)
  between operations  3.8 us (1%)
    pallas_call x1, Pallas kernels, reduce_scatter(): pl.pallas_call(functools.partial(reduce_kernel, counts), out_shape=(*(jax...  110 us
    ppermute x5, waiting for transfers between devices, send(): return lax.ppermute(value, 'section', [(0, 1)] if steps > 0 else [(1, 0)])  87 us
    pallas_call x2, Pallas kernels, attn_fwd(): pl.pallas_call(functools.partial(attn_fwd_kernel, same), out_shape=(jax.S...  30 us
    pallas_call x2, Pallas kernels, ffn_fwd(): pl.pallas_call(ffn_fwd_kernel, out_shape=(jax.ShapeDtypeStruct((s, d), BF...  26.9 us
    pallas_call x2, Pallas kernels, ffn_bwd(): pl.pallas_call(functools.partial(ffn_bwd_kernel, extra), out_shape=(jax.S...  24 us
    another operation x2, loops' own time, cross(): return lax.cond(decoder, decode, encode)  12.1 us
    pallas_call x1, Pallas kernels, attn_bwd(): pl.pallas_call(attn_bwd_kernel, out_shape=(jax.ShapeDtypeStruct((s, d), F...  10.6 us
    unnamed x53, local copies, waits for them, and re-layouts  9.94 us
  transfers between devices with their start and end apart: 5, of which 2 were waited for; matrix products, arithmetic and copies ran while one was open for 2% of the time, Pallas kernels for 11%

profile of v1, /device:TPU:0, one launch (start us, length us, event | category | flops | bytes accessed | tf_op | source)
XLA Modules:
  0.0 353.0 jit_solution(18312230431859037608)
XLA Ops:
  4.0 9.8 %shard_map.263 = (bf16[256,2304]{1,0:T(8,128)(2,1)}, bf16[256,768]{1,0:T(8,128)(2,1)}, f32[256,768]{1,0:T(8,128)}, f32[256,768]{1,0:T(8,128)}, f32[256,128]{1,0:T(8,128)}, /*index=5*/f32[256,768]{1,0:T(8,128)S(1)}) custom-call(s32[1,1]{1,0:T(1,128)} %bitcast.12.len_ref, bf16[256,768]{1,0:T(8,128)(2,1)} %bitcast.77, bf16[256,768]{1,0:T(8,128)(2,1)} %bitcast.78, ...), custom_call_target="tpu_custom_call" | custom-call | tf_op jit(solution)/shard_map/pallas_call | solution.py:110
  13.9 9.8 %conditional.9 = ((bf16[256,768]{1,0:T(8,128)(2,1)}, bf16[256,3072]{1,0:T(8,128)(2,1)}, bf16[256,3072]{1,0:T(8,128)(2,1)}, f32[256,768]{1,0:T(8,128)}, f32[256,128]{1,0:T(8,128)})) conditional(s32[]{:T(128)} %convert_element_type.2, (f32[256,768]{1,0:T(8,128)S(1)}, bf16[768,3072]{1,0:T(8,128)(2,1)}, bf16[3072,768]{1,0:T(8,128)(2,1)}, ...), branch_computations={%region_0.1_spmd, %region_1.2_spmd} | conditional | bytes 8 | solution.py:814
  13.9 9.8 %branch_0_fun.11 = (bf16[256,768]{1,0:T(8,128)(2,1)}, bf16[256,3072]{1,0:T(8,128)(2,1)}, bf16[256,3072]{1,0:T(8,128)(2,1)}, f32[256,768]{1,0:T(8,128)}, f32[256,128]{1,0:T(8,128)}) custom-call(f32[256,768]{1,0:T(8,128)S(1)} %get-tuple-element.224.n_ref, bf16[768,3072]{1,0:T(8,128)(2,1)} %get-tuple-element.225.we_ref, ...), custom_call_target="tpu_custom_call" | custom-call | tf_op jit(solution)/shard_map/cond/branch_0_fun/pallas_call | solution.py:274
  26.9 20.2 %shard_map.264 = (bf16[640,2304]{1,0:T(8,128)(2,1)}, bf16[640,768]{1,0:T(8,128)(2,1)}, f32[640,768]{1,0:T(8,128)}, f32[640,768]{1,0:T(8,128)}, f32[640,128]{1,0:T(8,128)}, /*index=5*/f32[640,768]{1,0:T(8,128)S(1)}) custom-call(s32[1,1]{1,0:T(1,128)} %bitcast.8.len_ref.refs_0_, bf16[640,768]{1,0:T(8,128)(2,1)} %bitcast.73, bf16[640,768]{1,0:T(8,128)(2,1)} %bitcast.74, ...), custom_call_target="tpu_custom_call" | custom-call | tf_op jit(solution)/shard_map/pallas_call | solution.py:110
  47.9 17.4 %conditional.10 = ((bf16[640,768]{1,0:T(8,128)(2,1)}, bf16[640,3072]{1,0:T(8,128)(2,1)}, bf16[640,3072]{1,0:T(8,128)(2,1)}, f32[640,768]{1,0:T(8,128)}, f32[640,128]{1,0:T(8,128)})) conditional(s32[]{:T(128)} %convert_element_type.2, (f32[640,768]{1,0:T(8,128)S(1)}, bf16[768,3072]{1,0:T(8,128)(2,1)}, bf16[3072,768]{1,0:T(8,128)(2,1)}, ...), branch_computations={%region_2.3_spmd, %region_3.4_spmd} | conditional | bytes 8 | solution.py:814
  48.1 17.1 %branch_0_fun.12 = (bf16[640,768]{1,0:T(8,128)(2,1)}, bf16[640,3072]{1,0:T(8,128)(2,1)}, bf16[640,3072]{1,0:T(8,128)(2,1)}, f32[640,768]{1,0:T(8,128)}, f32[640,128]{1,0:T(8,128)}) custom-call(f32[640,768]{1,0:T(8,128)S(1)} %get-tuple-element.230.n_ref, bf16[768,3072]{1,0:T(8,128)(2,1)} %get-tuple-element.231.we_ref, ...), custom_call_target="tpu_custom_call" | custom-call | tf_op jit(solution)/shard_map/cond/branch_0_fun/pallas_call | solution.py:274
  65.3 2.2 collective-permute-start.1
  69.8 19.0 %collective-permute-done.1 = bf16[640,768]{1,0:T(8,128)(2,1)} collective-permute-done((bf16[640,768]{1,0:T(8,128)(2,1)}, bf16[640,768]{1,0:T(8,128)(2,1)}, u32[]{:S(2)}, u32[]{:S(2)}) %collective-permute-start.1) | collective-permute-done | bytes 983072 | tf_op jit(solution)/shard_map/ppermute | solution.py:817
  88.8 12.0 %conditional.13 = ((bf16[640,2304]{1,0:T(8,128)(2,1)}, bf16[640,768]{1,0:T(8,128)(2,1)}, f32[640,768]{1,0:T(8,128)}, f32[640,768]{1,0:T(8,128)}, f32[640,128]{1,0:T(8,128)}, /*index=5*/f32[640,768]{1,0:T(8,128)})) conditional(s32[]{:T(128)} %convert_element_type.2, () %tuple.92, (s32[1,1]{1,0:T(1,128)}, f32[640,768]{1,0:T(8,128)S(1)}, ...), branch_computations={%region_8.9_spmd, %region_9.10_spmd} | conditional | bytes 8 | solution.py:830
  100.9 7.0 %conditional.14 = ((bf16[640,3072]{1,0:T(8,128)(2,1)}, bf16[640,3072]{1,0:T(8,128)(2,1)}, bf16[640,768]{1,0:T(8,128)(2,1)}, bf16[640,2304]{1,0:T(8,128)(2,1)}, b...) conditional(s32[]{:T(128)} %convert_element_type.2, () %tuple.91, ...), branch_computations={%region_10.11_spmd, %region_11.12_spmd} | conditional | bytes 1310844 | solution.py:857
  109.2 1.8 select_bitcast_fusion.1
  111.1 1.4 add.21
  113.7 2.3 select_bitcast_fusion
  116.0 9.5 %conditional.15 = ((f32[256,768]{1,0:T(8,128)}, bf16[256,3072]{1,0:T(8,128)(2,1)}, bf16[256,768]{1,0:T(8,128)(2,1)}, f32[8,768]{1,0:T(8,128)}, f32[1,3072]{1,0:T(1,128)})) conditional(s32[]{:T(128)} %convert_element_type.2, (s32[1,1]{1,0:T(1,128)}, bf16[256,768]{1,0:T(8,128)(2,1)S(1)}, bf16[256,768]{1,0:T(8,128)(2,1)}, ...), branch_computations={%region_12.13_spmd, %region_13.14_spmd} | conditional | bytes 48 | solution.py:905
  116.0 9.5 %branch_0_fun.17 = (f32[256,768]{1,0:T(8,128)}, bf16[256,3072]{1,0:T(8,128)(2,1)}, bf16[256,768]{1,0:T(8,128)(2,1)}, f32[8,768]{1,0:T(8,128)}, f32[1,3072]{1,0:T(1,128)}) custom-call(s32[1,1]{1,0:T(1,128)} %get-tuple-element.321.len_ref, bf16[256,768]{1,0:T(8,128)(2,1)S(1)} %get-tuple-element.322.cot_ref, bf16[256,768]{1,0:T(8,128)(2,1)} %get-tuple-element.323.dm_ref, ...), custom_call_target="tpu_custom_call" | custom-call | tf_op jit(solution)/shard_map/cond/branch_0_fun/pallas_call | solution.py:324
  125.6 10.6 %shard_map.265 = (f32[256,768]{1,0:T(8,128)}, bf16[256,2304]{1,0:T(8,128)(2,1)}, bf16[256,768]{1,0:T(8,128)(2,1)}, bf16[8,128]{1,0:T(8,128)(2,1)}, f32[8,768]{1,0:T(8,128)}) custom-call(s32[1,1]{1,0:T(1,128)} %bitcast.12.len_ref, f32[256,768]{1,0:T(8,128)} %get-tuple-element.511.dn_ref, bf16[256,2304]{1,0:T(8,128)(2,1)} %get-tuple-element.512.qkv_hbm, ...), custom_call_target="tpu_custom_call" | custom-call | tf_op jit(solution)/shard_map/pallas_call | solution.py:225
  136.1 68.0 %collective-permute-done.4 = f32[8,768]{1,0:T(8,128)} collective-permute-done((f32[8,768]{1,0:T(8,128)}, f32[8,768]{1,0:T(8,128)}, u32[]{:S(2)}, u32[]{:S(2)}) %collective-permute-start.4) | collective-permute-done | bytes 24608 | tf_op jit(solution)/shard_map/ppermute | solution.py:817
  204.2 1.3 broadcast_select_fusion.refs_29_
  205.6 24.5 %conditional.16 = (f32[640,768]{1,0:T(8,128)}, bf16[640,3072]{1,0:T(8,128)(2,1)}, f32[8,768]{1,0:T(8,128)}, f32[1,3072]{1,0:T(1,128)}, bf16[8,2,2,2,2,48,384]{6,5,4,3,2,1,0:T(8,128)(2,1)}) conditional(s32[]{:T(128)} %convert_element_type.2, (s32[1,1]{1,0:T(1,128)}, bf16[640,768]{1,0:T(8,128)(2,1)}, bf16[640,768]{1,0:T(8,128)(2,1)}, ...), branch_computations={%region_14.15_spmd, %region_15.16_spmd} | conditional | flops 9216 | bytes 11907196 | solution.py:929
  205.7 14.6 %branch_0_fun.18 = (f32[640,768]{1,0:T(8,128)}, bf16[640,3072]{1,0:T(8,128)(2,1)}, bf16[640,768]{1,0:T(8,128)(2,1)}, f32[8,768]{1,0:T(8,128)}, f32[1,3072]{1,0:T(1,128)}) custom-call(s32[1,1]{1,0:T(1,128)} %get-tuple-element.334.len_ref, bf16[640,768]{1,0:T(8,128)(2,1)} %get-tuple-element.335.cot_ref, bf16[640,768]{1,0:T(8,128)(2,1)} %get-tuple-element.336.dm_ref, ...), custom_call_target="tpu_custom_call" | custom-call | tf_op jit(solution)/shard_map/cond/branch_0_fun/pallas_call | solution.py:324
  220.4 8.5 %branch_0_fun.19 = bf16[8,16,48,384]{3,2,1,0:T(8,128)(2,1)} custom-call(bf16[256,3072]{1,0:T(8,128)(2,1)} %get-tuple-element.349.refs_0_, bf16[640,3072]{1,0:T(8,128)(2,1)S(1)} %get-tuple-element.350.refs_1_, bf16[256,768]{1,0:T(8,128)(2,1)} %get-tuple-element.351.refs_2_, bf16[640,768]{1,0:T(8,128)(2,1)} %get-tuple-element.352.refs_3_), custom_call_target="tpu_custom_call" | custom-call | tf_op jit(solution)/shard_map/cond/branch_0_fun/pallas_call | solution.py:370
  230.0 110.5 %shard_map.266 = (f32[640,768]{1,0:T(8,128)}, f32[48,2304]{1,0:T(8,128)}, f32[48,768]{1,0:T(8,128)}, f32[48,3072]{1,0:T(8,128)}, f32[192,768]{1,0:T(8,128)}, /*i...) custom-call(s32[1,1]{1,0:T(1,128)} %bitcast.8.len_ref.refs_0_, ...), custom_call_target="tpu_custom_call" | custom-call | tf_op jit(solution)/shard_map/pallas_call | solution.py:725
  342.6 1.4 fusion
  345.9 3.0 copy.161
  (82 shorter events, 18.6 us)
Async XLA Ops:
  2.7 44.4 %copy-start.7 = (f32[1,6,768]{2,1,0:T(8,128)}, f32[1,6,768]{2,1,0:T(8,128)S(1)}, u32[]{:S(2)}) copy-start(f32[1,6,768]{2,1,0:T(8,128)S(1)} %copy.42) | copy-start | bytes 55300
  4.0 9.8 %copy-start.6 = (f32[1,2,768]{2,1,0:T(2,128)S(1)}, f32[1,2,768]{2,1,0:T(2,128)}, u32[]{:S(2)}) copy-start(f32[1,2,768]{2,1,0:T(2,128)} %param.46) | copy-start | bytes 18436
  4.0 9.8 %copy-start.15 = (f32[1,3072]{1,0:T(1,128)S(1)}, f32[1,3072]{1,0:T(1,128)}, u32[]{:S(2)}) copy-start(f32[1,3072]{1,0:T(1,128)} %param.44) | copy-start | bytes 36868
  13.8 111.6 %copy-start.1 = (f32[256,768]{1,0:T(8,128)}, f32[256,768]{1,0:T(8,128)S(1)}, u32[]{:S(2)}) copy-start(f32[256,768]{1,0:T(8,128)S(1)} %get-tuple-element.484.refs_18_) | copy-start | bytes 2359300
  13.8 11.1 %copy-start.28 = (s32[2,1]{0,1:T(1,128)S(1)}, s32[2,1]{0,1:T(1,128)}, u32[]{:S(2)}) copy-start(s32[2,1]{0,1:T(1,128)} %param.38) | copy-start | bytes 28
  23.7 23.5 %collective-permute-start = (bf16[256,768]{1,0:T(8,128)(2,1)}, bf16[256,768]{1,0:T(8,128)(2,1)S(1)}, u32[]{:S(2)}, u32[]{:S(2)}) collective-permute-start(bf16[256,768]{1,0:T(8,128)(2,1)} %get-tuple-element.479), channel_id=1, source_target_pairs={{0,16},{1,17},{2,18},{3,19},{4,20},{5,21},{6,22},{7,23},{8,24},{9,... | collective-permute-start | bytes 1179656 | tf_op jit(solution)/shard_map/ppermute | solution.py:817
  47.1 78.3 %copy-start = (f32[640,768]{1,0:T(8,128)}, f32[640,768]{1,0:T(8,128)S(1)}, u32[]{:S(2)}) copy-start(f32[640,768]{1,0:T(8,128)S(1)} %get-tuple-element.493.refs_19_) | copy-start | bytes 5898244
  47.1 20.4 %copy-start.27 = (f32[768]{0:T(1024)S(1)}, f32[768]{0:T(1024)}, u32[]{:S(2)}) copy-start(f32[768]{0:T(1024)} %param.49) | copy-start | bytes 9220
  65.3 23.5 %collective-permute-start.1 = (bf16[640,768]{1,0:T(8,128)(2,1)}, bf16[640,768]{1,0:T(8,128)(2,1)}, u32[]{:S(2)}, u32[]{:S(2)}) collective-permute-start(bf16[640,768]{1,0:T(8,128)(2,1)} %get-tuple-element.483), channel_id=1, source_target_pairs={{0,16},{1,17},{2,18},{3,19},{4,20},{5,21},{6,22},{7,23},{8,24},{9,... | collective-permute-start | bytes 2949128 | tf_op jit(solution)/shard_map/ppermute | solution.py:817
  68.5 32.3 %collective-permute-start.2 = (bf16[256,768]{1,0:T(8,128)(2,1)}, bf16[256,768]{1,0:T(8,128)(2,1)}, u32[]{:S(2)}, u32[]{:S(2)}) collective-permute-start(bf16[256,768]{1,0:T(8,128)(2,1)} %get-tuple-element.492), channel_id=1, source_target_pairs={{16,0},{17,1},{18,2},{19,3},{20,4},{21,5},{22,6},{23,7},{24,8},{25... | collective-permute-start | bytes 1179656 | tf_op jit(solution)/shard_map/ppermute | solution.py:817
  107.9 96.3 %collective-permute-start.3 = (bf16[640,768]{1,0:T(8,128)(2,1)}, bf16[640,768]{1,0:T(8,128)(2,1)}, u32[]{:S(2)}, u32[]{:S(2)}) collective-permute-start(bf16[640,768]{1,0:T(8,128)(2,1)} %get-tuple-element.503), channel_id=1, source_target_pairs={{16,0},{17,1},{18,2},{19,3},{20,4},{21,5},{22,6},{23,7},{24,8},{25... | collective-permute-start | bytes 2949128 | tf_op jit(solution)/shard_map/ppermute | solution.py:817
  109.2 6.8 %copy-start.18 = (f32[256,128]{1,0:T(8,128)S(1)}, f32[256,128]{1,0:T(8,128)}, u32[]{:S(2)}) copy-start(f32[256,128]{1,0:T(8,128)} %get-tuple-element.509) | copy-start | bytes 393220
  112.4 91.7 %collective-permute-start.4 = (f32[8,768]{1,0:T(8,128)}, f32[8,768]{1,0:T(8,128)}, u32[]{:S(2)}, u32[]{:S(2)}) collective-permute-start(f32[8,768]{1,0:T(8,128)} %add.21), channel_id=1, source_target_pairs={{16,0},{17,1},{18,2},{19,3},{20,4},{21,5},{22,6},{23,7},{24,8},{25... | collective-permute-start | bytes 73736 | tf_op jit(solution)/shard_map/ppermute | solution.py:817
  125.5 80.0 %copy-start.2 = (bf16[640,3072]{1,0:T(8,128)(2,1)S(1)}, bf16[640,3072]{1,0:T(8,128)(2,1)}, u32[]{:S(2)}) copy-start(bf16[640,3072]{1,0:T(8,128)(2,1)} %get-tuple-element.525) | copy-start | bytes 11796484
  125.5 80.0 %copy-start.19 = (f32[8,768]{1,0:T(8,128)S(1)}, f32[8,768]{1,0:T(8,128)}, u32[]{:S(2)}) copy-start(f32[8,768]{1,0:T(8,128)} %get-tuple-element.527) | copy-start | bytes 73732
  125.5 80.0 %copy-start.20 = (f32[8,768]{1,0:T(8,128)S(1)}, f32[8,768]{1,0:T(8,128)}, u32[]{:S(2)}) copy-start(f32[8,768]{1,0:T(8,128)} %get-tuple-element.528) | copy-start | bytes 73732
  125.5 80.0 %copy-start.22 = (f32[8,768]{1,0:T(8,128)S(1)}, f32[8,768]{1,0:T(8,128)}, u32[]{:S(2)}) copy-start(f32[8,768]{1,0:T(8,128)} %get-tuple-element.522) | copy-start | bytes 73732
  125.5 80.0 %copy-start.23 = (f32[1,3072]{1,0:T(1,128)S(1)}, f32[1,3072]{1,0:T(1,128)}, u32[]{:S(2)}) copy-start(f32[1,3072]{1,0:T(1,128)} %get-tuple-element.529) | copy-start | bytes 36868
  125.5 80.0 %copy-start.24 = (f32[1,3072]{1,0:T(1,128)S(1)}, f32[1,3072]{1,0:T(1,128)}, u32[]{:S(2)}) copy-start(f32[1,3072]{1,0:T(1,128)} %get-tuple-element.530) | copy-start | bytes 36868
  125.6 80.0 %copy-start.26 = (f32[1,3072]{1,0:T(1,128)S(1)}, f32[1,3072]{1,0:T(1,128)}, u32[]{:S(2)}) copy-start(f32[1,3072]{1,0:T(1,128)} %get-tuple-element.523) | copy-start | bytes 36868
  220.3 8.5 %copy-start.25 = (f32[1,3072]{1,0:T(1,128)S(1)}, f32[1,3072]{1,0:T(1,128)}, u32[]{:S(2)}) copy-start(f32[1,3072]{1,0:T(1,128)} %get-tuple-element.348) | copy-start | bytes 36868 | tf_op jit(solution)/shard_map/cond
  220.3 9.1 %copy-start.21 = (f32[8,768]{1,0:T(8,128)S(1)}, f32[8,768]{1,0:T(8,128)}, u32[]{:S(2)}) copy-start(f32[8,768]{1,0:T(8,128)} %get-tuple-element.346) | copy-start | bytes 73732 | tf_op jit(solution)/shard_map/cond
  345.9 3.8 %copy-start.16 = (f32[48,768]{1,0:T(8,128)S(1)}, f32[48,768]{1,0:T(8,128)}, u32[]{:S(2)}) copy-start(f32[48,768]{1,0:T(8,128)} %get-tuple-element.561) | copy-start | bytes 442372
  345.9 4.5 %copy-start.10 = (f32[48,3072]{1,0:T(8,128)S(1)}, f32[48,3072]{1,0:T(8,128)}, u32[]{:S(2)}) copy-start(f32[48,3072]{1,0:T(8,128)} %get-tuple-element.562) | copy-start | bytes 1769476
  (5 other events, 10.1 us)

commit v2 on v1

--- a/solution.py
+++ b/solution.py
@@ -46,20 +46,35 @@
     xhat = c * r
     return xhat, r, xhat * gain + shift
 
+def incoming(sources, targets, sems):
+    return [pltpu.make_async_copy(src, dst, sems.at[k]) for k, (src, dst) in enumerate(zip(sources, targets))]
+
+
 def causal_shift(size):
     return jnp.where(lax.axis_index("section") == 1, 0, size)
 
 
-def attn_fwd_kernel(same, len_ref, xq_ref, xkv_ref, res_ref, wqkv_ref, wo_ref, bias_ref, gain_ref,
-                    qkv_ref, o_ref, lse_ref, xhat_ref, r_ref, n_ref):
+def attn_fwd_kernel(same, len_ref, xq_ref, *refs):
+    xkv_ref, refs = (xq_ref, refs) if same else (refs[0], refs[1:])
+    (w_hbm, wo_hbm, bias_ref, gain_ref, qkv_hbm, o_hbm, lse_hbm, xhat_ref, r_ref, n_ref) = refs[:10]
+    (qkv_ref, o_ref, lse_ref, w_ref, wo_ref, in_sems, out_sems) = refs[10:]
     s, d = xq_ref.shape
-    if not same:
-        wo_ref = wqkv_ref.at[:, 3 * d :]
+    parts = [slice(j * d, (j + 1) * d) for j in range(3)]
+    weights = incoming(
+        (*(w_hbm.at[:, part] for part in parts), wo_hbm.at[:, wo_hbm.shape[1] - d :]),
+        (*(w_ref.at[:, part] for part in parts), wo_ref),
+        in_sems,
+    )
+    results = incoming((qkv_ref, o_ref, lse_ref), (qkv_hbm, o_hbm, lse_hbm), out_sems)
+    for copy in weights:
+        copy.start()
     xq = xq_ref[...].astype(BF)
     xkv = xq if same else xkv_ref[...]
-    qkv_ref[:, :d] = (dot(xq, wqkv_ref[:, :d]) + bias_ref[0:1, :]).astype(BF)
-    qkv_ref[:, d:2*d] = dot(xkv, wqkv_ref[:, d:2*d]).astype(BF)
-    qkv_ref[:, 2*d:] = (dot(xkv, wqkv_ref[:, 2*d:3*d]) + bias_ref[1:2, :]).astype(BF)
+    for x, part, weight, shift in zip((xq, xkv, xkv), parts, weights, (bias_ref[0:1, :], None, bias_ref[1:2, :])):
+        weight.wait()
+        total = dot(x, w_ref[:, part])
+        qkv_ref[:, part] = (total if shift is None else total + shift).astype(BF)
+    results[0].start()
     length = len_ref[0, 0]
     lane = lanes(s)
     row = lax.broadcasted_iota(jnp.int32, (s, 128), 0)
@@ -92,28 +107,35 @@
         lse_ref[:, pl.ds(at, 128)] = jnp.where(lane < 64, lses[1], lses[0])
         return 0
     lax.fori_loop(0, d // 128, pair, 0)
-    u = res_ref[...].astype(F32) + dot(o_ref[...], wo_ref[...]) + bias_ref[2:3, :]
+    for copy in results[1:]:
+        copy.start()
+    weights[3].wait()
+    u = xq_ref[...].astype(F32) + dot(o_ref[...], wo_ref[...]) + bias_ref[2:3, :]
     xhat, r, n = norm_forward(u, gain_ref[0:1, :], bias_ref[3:4, :])
     xhat_ref[...] = xhat
     r_ref[...] = jnp.broadcast_to(r, r_ref.shape)
     n_ref[...] = n
-
-def attn_fwd(xq, xkv, res, wqkv, wo, bias, gain, length):
+    for copy in results:
+        copy.wait()
+
+
+def attn_fwd(xq, xkv, wqkv, wo, bias, gain, length):
     s, d = xq.shape
     same = xkv is None
-    if same:
-        xkv = xq
-    else:
-        wo = gain
     vm = pl.BlockSpec(memory_space=pltpu.VMEM)
     sm = pl.BlockSpec(memory_space=pltpu.SMEM)
+    hbm = pl.BlockSpec(memory_space=pl.ANY)
+    rows = (xq,) if same else (xq, xkv)
     return pl.pallas_call(
         functools.partial(attn_fwd_kernel, same),
         out_shape=(jax.ShapeDtypeStruct((s, 3 * d), BF), jax.ShapeDtypeStruct((s, d), BF), jax.ShapeDtypeStruct((s, d), F32),
                    jax.ShapeDtypeStruct((s, d), F32), jax.ShapeDtypeStruct((s, 128), F32), jax.ShapeDtypeStruct((s, d), F32)),
-        in_specs=[sm] + [vm] * 7, out_specs=(vm,) * 6,
+        in_specs=[sm] + [vm] * len(rows) + [hbm, hbm, vm, vm], out_specs=(hbm, hbm, hbm, vm, vm, vm),
+        scratch_shapes=[pltpu.VMEM((s, 3 * d), BF), pltpu.VMEM((s, d), BF), pltpu.VMEM((s, d), F32),
+                        pltpu.VMEM((d, 3 * d), BF), pltpu.VMEM((d, d), BF),
+                        pltpu.SemaphoreType.DMA((4,)), pltpu.SemaphoreType.DMA((3,))],
         compiler_params=pltpu.CompilerParams(vmem_limit_bytes=60 << 20),
-    )(length.reshape(1, 1), xq, xkv, res, wqkv, wo, bias, gain)
+    )(length.reshape(1, 1), *rows, wqkv, wqkv if wo is None else wo, bias, gain)
 
 def norm_backward(dn, xhat, r, gain):
     h = dn * gain
@@ -191,10 +213,6 @@
     sums_ref[0:1, :] = jnp.sum(dqkv_ref[:, :d].astype(F32), axis=0, keepdims=True)
     sums_ref[1:2, :] = jnp.sum(dqkv_ref[:, 2*d:].astype(F32), axis=0, keepdims=True)
     sums_ref[5:8, :] = jnp.zeros((3, d), F32)
-
-def incoming(sources, targets, sems):
-    return [pltpu.make_async_copy(src, dst, sems.at[k]) for k, (src, dst) in enumerate(zip(sources, targets))]
-
 
 def attn_bwd_kernel(len_ref, dn_ref, qkv_hbm, o_hbm, lse_hbm, xhat_ref, r_ref, w_hbm, wo_hbm, gain_ref,
                     dres_ref, dqkv_ref, dt_ref, dkvx_ref, sums_ref, do_ref, dq_ref, qkv_ref, o_ref, lse_ref, w_ref, wo_ref, sems):
@@ -803,7 +821,7 @@
 
     def attend(i):
         x = xs[i]
-        return attn_fwd(x, None, x, w_in, w_out, bias, gain, own[i])
+        return attn_fwd(x, None, w_in, w_out, bias, gain, own[i])
 
     def encode_ffn(i, n):
         s = sizes[i]
@@ -825,7 +843,7 @@
             )
 
         def decode():
-            return attn_fwd(n1, memory, n1, cross_weight, None, cross_biases, c_gain, source[i])
+            return attn_fwd(n1, memory, cross_weight, None, cross_biases, c_gain, source[i])
 
         return lax.cond(decoder, decode, encode)
 

time: 355 us -> 356 us (level)
    unnamed x53 -> x51, local copies, waits for them, and re-layouts: 9.94 us -> 9.19 us
where the time goes in v2:
time: 356 us; the launch traced here: 354 us
  Pallas kernels  211 us (59%)
  waiting for transfers between devices  87.7 us (25%)
  loops' own time  19.9 us (6%)
  local copies, waits for them, and re-layouts  15.9 us (4%)
  other arithmetic  8.03 us (2%)
  starting transfers between devices  7.4 us (2%)
  between operations  3.84 us (1%)
    pallas_call x1, Pallas kernels, reduce_scatter(): pl.pallas_call(functools.partial(reduce_kernel, counts), out_shape=(*(jax...  110 us
    ppermute x5, waiting for transfers between devices, send(): return lax.ppermute(value, 'section', [(0, 1)] if steps > 0 else [(1, 0)])  87.7 us
    pallas_call x2, Pallas kernels, attn_fwd(): pl.pallas_call(functools.partial(attn_fwd_kernel, same), out_shape=(jax.S...  30.6 us
    pallas_call x2, Pallas kernels, ffn_fwd(): pl.pallas_call(ffn_fwd_kernel, out_shape=(jax.ShapeDtypeStruct((s, d), BF...  27.3 us
    pallas_call x2, Pallas kernels, ffn_bwd(): pl.pallas_call(functools.partial(ffn_bwd_kernel, extra), out_shape=(jax.S...  24 us
    another operation x2, loops' own time, cross(): return lax.cond(decoder, decode, encode)  12.4 us
    pallas_call x1, Pallas kernels, attn_bwd(): pl.pallas_call(attn_bwd_kernel, out_shape=(jax.ShapeDtypeStruct((s, d), F...  10.6 us
    unnamed x51, local copies, waits for them, and re-layouts  9.19 us
  transfers between devices with their start and end apart: 5, of which 2 were waited for; matrix products, arithmetic and copies ran while one was open for 2% of the time, Pallas kernels for 11%

profile of v2, /device:TPU:0, one launch (start us, length us, event | category | flops | bytes accessed | tf_op | source)
XLA Modules:
  0.0 353.9 jit_solution(16710272012100920908)
XLA Ops:
  4.0 10.1 %shard_map.263 = (bf16[256,2304]{1,0:T(8,128)(2,1)}, bf16[256,768]{1,0:T(8,128)(2,1)}, f32[256,768]{1,0:T(8,128)}, f32[256,768]{1,0:T(8,128)}, f32[256,128]{1,0:T(8,128)}, /*index=5*/f32[256,768]{1,0:T(8,128)S(1)}) custom-call(s32[1,1]{1,0:T(1,128)} %bitcast.12.len_ref, bf16[256,768]{1,0:T(8,128)(2,1)} %bitcast.78, bf16[768,2304]{1,0:T(8,128)(2,1)} %bitcast.63, ...), custom_call_target="tpu_custom_call" | custom-call | tf_op jit(solution)/shard_map/pallas_call | solution.py:129
  14.2 9.8 %conditional.9 = ((bf16[256,768]{1,0:T(8,128)(2,1)}, bf16[256,3072]{1,0:T(8,128)(2,1)}, bf16[256,3072]{1,0:T(8,128)(2,1)}, f32[256,768]{1,0:T(8,128)}, f32[256,128]{1,0:T(8,128)})) conditional(s32[]{:T(128)} %convert_element_type.2, (f32[256,768]{1,0:T(8,128)S(1)}, bf16[768,3072]{1,0:T(8,128)(2,1)}, bf16[3072,768]{1,0:T(8,128)(2,1)}, ...), branch_computations={%region_0.1_spmd, %region_1.2_spmd} | conditional | bytes 8 | solution.py:832
  14.2 9.8 %branch_0_fun.11 = (bf16[256,768]{1,0:T(8,128)(2,1)}, bf16[256,3072]{1,0:T(8,128)(2,1)}, bf16[256,3072]{1,0:T(8,128)(2,1)}, f32[256,768]{1,0:T(8,128)}, f32[256,128]{1,0:T(8,128)}) custom-call(f32[256,768]{1,0:T(8,128)S(1)} %get-tuple-element.224.n_ref, bf16[768,3072]{1,0:T(8,128)(2,1)} %get-tuple-element.225.we_ref, ...), custom_call_target="tpu_custom_call" | custom-call | tf_op jit(solution)/shard_map/cond/branch_0_fun/pallas_call | solution.py:292
  27.2 20.5 %shard_map.264 = (bf16[640,2304]{1,0:T(8,128)(2,1)}, bf16[640,768]{1,0:T(8,128)(2,1)}, f32[640,768]{1,0:T(8,128)}, f32[640,768]{1,0:T(8,128)}, f32[640,128]{1,0:T(8,128)}, /*index=5*/f32[640,768]{1,0:T(8,128)S(1)}) custom-call(s32[1,1]{1,0:T(1,128)} %bitcast.8.len_ref.refs_0_, bf16[640,768]{1,0:T(8,128)(2,1)} %bitcast.73, bf16[768,2304]{1,0:T(8,128)(2,1)} %bitcast.64, ...), custom_call_target="tpu_custom_call" | custom-call | tf_op jit(solution)/shard_map/pallas_call | solution.py:129
  47.8 17.8 %conditional.10 = ((bf16[640,768]{1,0:T(8,128)(2,1)}, bf16[640,3072]{1,0:T(8,128)(2,1)}, bf16[640,3072]{1,0:T(8,128)(2,1)}, f32[640,768]{1,0:T(8,128)}, f32[640,128]{1,0:T(8,128)})) conditional(s32[]{:T(128)} %convert_element_type.2, (f32[640,768]{1,0:T(8,128)S(1)}, bf16[768,3072]{1,0:T(8,128)(2,1)}, bf16[3072,768]{1,0:T(8,128)(2,1)}, ...), branch_computations={%region_2.3_spmd, %region_3.4_spmd} | conditional | bytes 8 | solution.py:832
  48.1 17.5 %branch_0_fun.12 = (bf16[640,768]{1,0:T(8,128)(2,1)}, bf16[640,3072]{1,0:T(8,128)(2,1)}, bf16[640,3072]{1,0:T(8,128)(2,1)}, f32[640,768]{1,0:T(8,128)}, f32[640,128]{1,0:T(8,128)}) custom-call(f32[640,768]{1,0:T(8,128)S(1)} %get-tuple-element.230.n_ref, bf16[768,3072]{1,0:T(8,128)(2,1)} %get-tuple-element.231.we_ref, ...), custom_call_target="tpu_custom_call" | custom-call | tf_op jit(solution)/shard_map/cond/branch_0_fun/pallas_call | solution.py:292
  65.6 2.2 collective-permute-start.1
  70.1 19.0 %collective-permute-done.1 = bf16[640,768]{1,0:T(8,128)(2,1)} collective-permute-done((bf16[640,768]{1,0:T(8,128)(2,1)}, bf16[640,768]{1,0:T(8,128)(2,1)}, u32[]{:S(2)}, u32[]{:S(2)}) %collective-permute-start.1) | collective-permute-done | bytes 983072 | tf_op jit(solution)/shard_map/ppermute | solution.py:835
  89.1 12.4 %conditional.13 = ((bf16[640,2304]{1,0:T(8,128)(2,1)}, bf16[640,768]{1,0:T(8,128)(2,1)}, f32[640,768]{1,0:T(8,128)}, f32[640,768]{1,0:T(8,128)}, f32[640,128]{1,0:T(8,128)}, /*index=5*/f32[640,768]{1,0:T(8,128)})) conditional(s32[]{:T(128)} %convert_element_type.2, () %tuple.92, (s32[1,1]{1,0:T(1,128)}, f32[640,768]{1,0:T(8,128)S(1)}, ...), branch_computations={%region_8.9_spmd, %region_9.10_spmd} | conditional | bytes 8 | solution.py:848
  101.5 7.0 %conditional.14 = ((bf16[640,3072]{1,0:T(8,128)(2,1)}, bf16[640,3072]{1,0:T(8,128)(2,1)}, bf16[640,768]{1,0:T(8,128)(2,1)}, bf16[640,2304]{1,0:T(8,128)(2,1)}, b...) conditional(s32[]{:T(128)} %convert_element_type.2, () %tuple.91, ...), branch_computations={%region_10.11_spmd, %region_11.12_spmd} | conditional | bytes 1310844 | solution.py:875
  109.9 1.8 select_bitcast_fusion.1
  111.7 1.4 add.21
  114.4 2.3 select_bitcast_fusion
  116.6 9.5 %conditional.15 = ((f32[256,768]{1,0:T(8,128)}, bf16[256,3072]{1,0:T(8,128)(2,1)}, bf16[256,768]{1,0:T(8,128)(2,1)}, f32[8,768]{1,0:T(8,128)}, f32[1,3072]{1,0:T(1,128)})) conditional(s32[]{:T(128)} %convert_element_type.2, (s32[1,1]{1,0:T(1,128)}, bf16[256,768]{1,0:T(8,128)(2,1)S(1)}, bf16[256,768]{1,0:T(8,128)(2,1)}, ...), branch_computations={%region_12.13_spmd, %region_13.14_spmd} | conditional | bytes 48 | solution.py:923
  116.6 9.5 %branch_0_fun.17 = (f32[256,768]{1,0:T(8,128)}, bf16[256,3072]{1,0:T(8,128)(2,1)}, bf16[256,768]{1,0:T(8,128)(2,1)}, f32[8,768]{1,0:T(8,128)}, f32[1,3072]{1,0:T(1,128)}) custom-call(s32[1,1]{1,0:T(1,128)} %get-tuple-element.321.len_ref, bf16[256,768]{1,0:T(8,128)(2,1)S(1)} %get-tuple-element.322.cot_ref, bf16[256,768]{1,0:T(8,128)(2,1)} %get-tuple-element.323.dm_ref, ...), custom_call_target="tpu_custom_call" | custom-call | tf_op jit(solution)/shard_map/cond/branch_0_fun/pallas_call | solution.py:342
  126.2 10.6 %shard_map.265 = (f32[256,768]{1,0:T(8,128)}, bf16[256,2304]{1,0:T(8,128)(2,1)}, bf16[256,768]{1,0:T(8,128)(2,1)}, bf16[8,128]{1,0:T(8,128)(2,1)}, f32[8,768]{1,0:T(8,128)}) custom-call(s32[1,1]{1,0:T(1,128)} %bitcast.12.len_ref, f32[256,768]{1,0:T(8,128)} %get-tuple-element.511.dn_ref, bf16[256,2304]{1,0:T(8,128)(2,1)} %get-tuple-element.512.qkv_hbm, ...), custom_call_target="tpu_custom_call" | custom-call | tf_op jit(solution)/shard_map/pallas_call | solution.py:243
  136.8 68.7 %collective-permute-done.4 = f32[8,768]{1,0:T(8,128)} collective-permute-done((f32[8,768]{1,0:T(8,128)}, f32[8,768]{1,0:T(8,128)}, u32[]{:S(2)}, u32[]{:S(2)}) %collective-permute-start.4) | collective-permute-done | bytes 24608 | tf_op jit(solution)/shard_map/ppermute | solution.py:835
  205.5 1.3 broadcast_select_fusion.refs_29_
  206.8 24.5 %conditional.16 = (f32[640,768]{1,0:T(8,128)}, bf16[640,3072]{1,0:T(8,128)(2,1)}, f32[8,768]{1,0:T(8,128)}, f32[1,3072]{1,0:T(1,128)}, bf16[8,2,2,2,2,48,384]{6,5,4,3,2,1,0:T(8,128)(2,1)}) conditional(s32[]{:T(128)} %convert_element_type.2, (s32[1,1]{1,0:T(1,128)}, bf16[640,768]{1,0:T(8,128)(2,1)}, bf16[640,768]{1,0:T(8,128)(2,1)}, ...), branch_computations={%region_14.15_spmd, %region_15.16_spmd} | conditional | flops 9216 | bytes 11907196 | solution.py:947
  207.0 14.6 %branch_0_fun.18 = (f32[640,768]{1,0:T(8,128)}, bf16[640,3072]{1,0:T(8,128)(2,1)}, bf16[640,768]{1,0:T(8,128)(2,1)}, f32[8,768]{1,0:T(8,128)}, f32[1,3072]{1,0:T(1,128)}) custom-call(s32[1,1]{1,0:T(1,128)} %get-tuple-element.334.len_ref, bf16[640,768]{1,0:T(8,128)(2,1)} %get-tuple-element.335.cot_ref, bf16[640,768]{1,0:T(8,128)(2,1)} %get-tuple-element.336.dm_ref, ...), custom_call_target="tpu_custom_call" | custom-call | tf_op jit(solution)/shard_map/cond/branch_0_fun/pallas_call | solution.py:342
  221.6 8.5 %branch_0_fun.19 = bf16[8,16,48,384]{3,2,1,0:T(8,128)(2,1)} custom-call(bf16[256,3072]{1,0:T(8,128)(2,1)} %get-tuple-element.349.refs_0_, bf16[640,3072]{1,0:T(8,128)(2,1)S(1)} %get-tuple-element.350.refs_1_, bf16[256,768]{1,0:T(8,128)(2,1)} %get-tuple-element.351.refs_2_, bf16[640,768]{1,0:T(8,128)(2,1)} %get-tuple-element.352.refs_3_), custom_call_target="tpu_custom_call" | custom-call | tf_op jit(solution)/shard_map/cond/branch_0_fun/pallas_call | solution.py:388
  231.3 110.1 %shard_map.266 = (f32[640,768]{1,0:T(8,128)}, f32[48,2304]{1,0:T(8,128)}, f32[48,768]{1,0:T(8,128)}, f32[48,3072]{1,0:T(8,128)}, f32[192,768]{1,0:T(8,128)}, /*i...) custom-call(s32[1,1]{1,0:T(1,128)} %bitcast.8.len_ref.refs_0_, ...), custom_call_target="tpu_custom_call" | custom-call | tf_op jit(solution)/shard_map/pallas_call | solution.py:743
  343.5 1.4 fusion
  346.8 3.0 copy.161
  (80 shorter events, 17.9 us)
Async XLA Ops:
  2.7 45.1 %copy-start.7 = (f32[1,6,768]{2,1,0:T(8,128)}, f32[1,6,768]{2,1,0:T(8,128)S(1)}, u32[]{:S(2)}) copy-start(f32[1,6,768]{2,1,0:T(8,128)S(1)} %copy.42) | copy-start | bytes 55300
  4.0 10.2 %copy-start.6 = (f32[1,2,768]{2,1,0:T(2,128)S(1)}, f32[1,2,768]{2,1,0:T(2,128)}, u32[]{:S(2)}) copy-start(f32[1,2,768]{2,1,0:T(2,128)} %param.46) | copy-start | bytes 18436
  4.0 10.2 %copy-start.15 = (f32[1,3072]{1,0:T(1,128)S(1)}, f32[1,3072]{1,0:T(1,128)}, u32[]{:S(2)}) copy-start(f32[1,3072]{1,0:T(1,128)} %param.44) | copy-start | bytes 36868
  14.2 111.9 %copy-start.1 = (f32[256,768]{1,0:T(8,128)}, f32[256,768]{1,0:T(8,128)S(1)}, u32[]{:S(2)}) copy-start(f32[256,768]{1,0:T(8,128)S(1)} %get-tuple-element.484.refs_18_) | copy-start | bytes 2359300
  14.2 11.1 %copy-start.28 = (s32[2,1]{0,1:T(1,128)S(1)}, s32[2,1]{0,1:T(1,128)}, u32[]{:S(2)}) copy-start(s32[2,1]{0,1:T(1,128)} %param.38) | copy-start | bytes 28
  24.0 23.8 %collective-permute-start = (bf16[256,768]{1,0:T(8,128)(2,1)}, bf16[256,768]{1,0:T(8,128)(2,1)S(1)}, u32[]{:S(2)}, u32[]{:S(2)}) collective-permute-start(bf16[256,768]{1,0:T(8,128)(2,1)} %get-tuple-element.479), channel_id=1, source_target_pairs={{0,16},{1,17},{2,18},{3,19},{4,20},{5,21},{6,22},{7,23},{8,24},{9,... | collective-permute-start | bytes 1179656 | tf_op jit(solution)/shard_map/ppermute | solution.py:835
  47.7 78.4 %copy-start = (f32[640,768]{1,0:T(8,128)}, f32[640,768]{1,0:T(8,128)S(1)}, u32[]{:S(2)}) copy-start(f32[640,768]{1,0:T(8,128)S(1)} %get-tuple-element.493.refs_19_) | copy-start | bytes 5898244
  47.8 20.0 %copy-start.27 = (f32[768]{0:T(1024)S(1)}, f32[768]{0:T(1024)}, u32[]{:S(2)}) copy-start(f32[768]{0:T(1024)} %param.49) | copy-start | bytes 9220
  65.6 23.5 %collective-permute-start.1 = (bf16[640,768]{1,0:T(8,128)(2,1)}, bf16[640,768]{1,0:T(8,128)(2,1)}, u32[]{:S(2)}, u32[]{:S(2)}) collective-permute-start(bf16[640,768]{1,0:T(8,128)(2,1)} %get-tuple-element.483), channel_id=1, source_target_pairs={{0,16},{1,17},{2,18},{3,19},{4,20},{5,21},{6,22},{7,23},{8,24},{9,... | collective-permute-start | bytes 2949128 | tf_op jit(solution)/shard_map/ppermute | solution.py:835
  68.8 32.7 %collective-permute-start.2 = (bf16[256,768]{1,0:T(8,128)(2,1)}, bf16[256,768]{1,0:T(8,128)(2,1)}, u32[]{:S(2)}, u32[]{:S(2)}) collective-permute-start(bf16[256,768]{1,0:T(8,128)(2,1)} %get-tuple-element.492), channel_id=1, source_target_pairs={{16,0},{17,1},{18,2},{19,3},{20,4},{21,5},{22,6},{23,7},{24,8},{25... | collective-permute-start | bytes 1179656 | tf_op jit(solution)/shard_map/ppermute | solution.py:835
  108.6 96.9 %collective-permute-start.3 = (bf16[640,768]{1,0:T(8,128)(2,1)}, bf16[640,768]{1,0:T(8,128)(2,1)}, u32[]{:S(2)}, u32[]{:S(2)}) collective-permute-start(bf16[640,768]{1,0:T(8,128)(2,1)} %get-tuple-element.503), channel_id=1, source_target_pairs={{16,0},{17,1},{18,2},{19,3},{20,4},{21,5},{22,6},{23,7},{24,8},{25... | collective-permute-start | bytes 2949128 | tf_op jit(solution)/shard_map/ppermute | solution.py:835
  109.9 6.8 %copy-start.18 = (f32[256,128]{1,0:T(8,128)S(1)}, f32[256,128]{1,0:T(8,128)}, u32[]{:S(2)}) copy-start(f32[256,128]{1,0:T(8,128)} %get-tuple-element.509) | copy-start | bytes 393220
  113.1 92.4 %collective-permute-start.4 = (f32[8,768]{1,0:T(8,128)}, f32[8,768]{1,0:T(8,128)}, u32[]{:S(2)}, u32[]{:S(2)}) collective-permute-start(f32[8,768]{1,0:T(8,128)} %add.21), channel_id=1, source_target_pairs={{16,0},{17,1},{18,2},{19,3},{20,4},{21,5},{22,6},{23,7},{24,8},{25... | collective-permute-start | bytes 73736 | tf_op jit(solution)/shard_map/ppermute | solution.py:835
  126.2 80.6 %copy-start.2 = (bf16[640,3072]{1,0:T(8,128)(2,1)S(1)}, bf16[640,3072]{1,0:T(8,128)(2,1)}, u32[]{:S(2)}) copy-start(bf16[640,3072]{1,0:T(8,128)(2,1)} %get-tuple-element.525) | copy-start | bytes 11796484
  126.2 80.6 %copy-start.19 = (f32[8,768]{1,0:T(8,128)S(1)}, f32[8,768]{1,0:T(8,128)}, u32[]{:S(2)}) copy-start(f32[8,768]{1,0:T(8,128)} %get-tuple-element.527) | copy-start | bytes 73732
  126.2 80.6 %copy-start.20 = (f32[8,768]{1,0:T(8,128)S(1)}, f32[8,768]{1,0:T(8,128)}, u32[]{:S(2)}) copy-start(f32[8,768]{1,0:T(8,128)} %get-tuple-element.528) | copy-start | bytes 73732
  126.2 80.6 %copy-start.22 = (f32[8,768]{1,0:T(8,128)S(1)}, f32[8,768]{1,0:T(8,128)}, u32[]{:S(2)}) copy-start(f32[8,768]{1,0:T(8,128)} %get-tuple-element.522) | copy-start | bytes 73732
  126.2 80.6 %copy-start.23 = (f32[1,3072]{1,0:T(1,128)S(1)}, f32[1,3072]{1,0:T(1,128)}, u32[]{:S(2)}) copy-start(f32[1,3072]{1,0:T(1,128)} %get-tuple-element.529) | copy-start | bytes 36868
  126.2 80.6 %copy-start.24 = (f32[1,3072]{1,0:T(1,128)S(1)}, f32[1,3072]{1,0:T(1,128)}, u32[]{:S(2)}) copy-start(f32[1,3072]{1,0:T(1,128)} %get-tuple-element.530) | copy-start | bytes 36868
  126.2 80.6 %copy-start.26 = (f32[1,3072]{1,0:T(1,128)S(1)}, f32[1,3072]{1,0:T(1,128)}, u32[]{:S(2)}) copy-start(f32[1,3072]{1,0:T(1,128)} %get-tuple-element.523) | copy-start | bytes 36868
  221.6 8.5 %copy-start.25 = (f32[1,3072]{1,0:T(1,128)S(1)}, f32[1,3072]{1,0:T(1,128)}, u32[]{:S(2)}) copy-start(f32[1,3072]{1,0:T(1,128)} %get-tuple-element.348) | copy-start | bytes 36868 | tf_op jit(solution)/shard_map/cond
  221.6 9.1 %copy-start.21 = (f32[8,768]{1,0:T(8,128)S(1)}, f32[8,768]{1,0:T(8,128)}, u32[]{:S(2)}) copy-start(f32[8,768]{1,0:T(8,128)} %get-tuple-element.346) | copy-start | bytes 73732 | tf_op jit(solution)/shard_map/cond
  346.8 3.8 %copy-start.16 = (f32[48,768]{1,0:T(8,128)S(1)}, f32[48,768]{1,0:T(8,128)}, u32[]{:S(2)}) copy-start(f32[48,768]{1,0:T(8,128)} %get-tuple-element.561) | copy-start | bytes 442372
  346.8 4.5 %copy-start.10 = (f32[48,3072]{1,0:T(8,128)S(1)}, f32[48,3072]{1,0:T(8,128)}, u32[]{:S(2)}) copy-start(f32[48,3072]{1,0:T(8,128)} %get-tuple-element.562) | copy-start | bytes 1769476
  (4 other events, 9.4 us)

commit v3 on v1

--- a/solution.py
+++ b/solution.py
@@ -417,7 +417,8 @@
     (len_ref, dn_ref, qkv_hbm, o_hbm, lse_hbm, xhat_ref, r_ref, w_hbm, wo_ref, gain_ref) = refs[:10]
     (contract, cross_first, cross_second) = refs[15:18]
     ffn_refs = (refs[18:22], refs[22:26])
-    (ssum_ref, fsum_ref, esum_ref, csum_ref) = refs[26:30]
+    (ssum_ref, fsum_ref, esum_ref, csum_ref, csent_ref) = refs[26:31]
+    refs = (*refs[:30], *refs[31:])
     (dres_ref, in_ref, out_ref, expand_ref, contract_ref, cross_ref, vsum_ref, landed) = refs[30:38]
     (dqkv_ref, dt_ref, do_ref, dq_ref, sums_ref, made, own, r0, r1, r2, r3, vbuf, vrecv) = refs[38:51]
     (n0_buf, n1_buf, da0_buf, da1_buf) = refs[51:55]
@@ -673,7 +674,7 @@
     count = esum_ref.shape[1] // d
     for j in range(count):
         vbuf[0, 8 + j : 9 + j] = esum_ref[:, j * d : (j + 1) * d]
-    vbuf[0, 8 + count : 13 + count] = csum_ref[0:5, :]
+    vbuf[0, 8 + count : 13 + count] = jnp.where(second, csum_ref[0:5, :], csent_ref[0:5, :])
     vbuf[0, 13 + count :] = jnp.zeros((vbuf.shape[1] - 13 - count, d), F32)
     def weight(i, _):
         at = pl.ds(pl.multiple_of(i * d, 128), d)
@@ -725,7 +726,7 @@
     return pl.pallas_call(
         functools.partial(reduce_kernel, counts),
         out_shape=(*(jax.ShapeDtypeStruct(shape, F32) for shape in shapes), jax.ShapeDtypeStruct(parts[1].shape, BF)),
-        in_specs=[sm, vm, hbm, hbm, hbm, vm, vm, hbm, vm, vm] + [hbm] * 16 + [vm] * 4,
+        in_specs=[sm, vm, hbm, hbm, hbm, vm, vm, hbm, vm, vm] + [hbm] * 16 + [vm] * 5,
         out_specs=(*(vm,) * 7, hbm),
         scratch_shapes=[
             pltpu.VMEM((s, 3 * d), BF),
@@ -908,8 +909,8 @@
         lambda: tuple(ffn_bwd(cots[0], back0, source[0], ffn0[2:], w_e, w_c, gain)),
     )
     self0 = attn_bwd(dn0, att0[:5], w_in, w_out, gain, own[0], True)
-    back1, cross_sent, _ = lax.optimization_barrier((back1, send(cross_sums, -1), self0[0]))
-    cross_rows = jnp.where(decoder, cross_sums, cross_sent)
+    cross_sent = send(cross_sums, -1)
+    back1, _ = lax.optimization_barrier((back1, self0[0]))
 
     def plain(left, right):
         left, right = (jnp.concatenate([e.astype(BF) for e in side], 0) for side in (left, right))
@@ -933,12 +934,13 @@
             (g_contract, cross_first, cross_second),
             (att0[5], att1[5], enc0[0], enc_da),
             (out0[5], out1[5], keep0[1], keep1[1]),
-            (self0[4], ffn_sums, sum_e, cross_rows),
+            (self0[4], ffn_sums, sum_e, cross_sums, cross_sent),
         )
     else:
         self1 = attn_bwd(dn1, att1[:5], w_in, w_out, gain, own[1], True)
         dx1 = self1[0]
         self_sums = self0[4] + self1[4]
+        cross_rows = jnp.where(decoder, cross_sums, cross_sent)
         rows = [self_sums[0:4], ffn_sums[0:2], self_sums[4:5], ffn_sums[2:3], sum_e.reshape(ff // d, d), cross_rows[0:5]]
         rows = lax.psum(jnp.concatenate(rows, 0), "dp")
         cross_mine = jnp.where(decoder, cross_second, send(cross_first, -1))

time: 355 us -> 354 us (level)
  transfers between devices with their start and end apart: 5 -> 5, of which waited for: 2 -> 2; matrix products, arithmetic and copies ran while one was open for 2% -> 2% of each run, Pallas kernels for 11% -> 18%
where the time goes in v3:
time: 354 us; the launch traced here: 352 us
  Pallas kernels  211 us (60%)
  waiting for transfers between devices  86.8 us (25%)
  loops' own time  19.5 us (6%)
  local copies, waits for them, and re-layouts  16.6 us (5%)
  starting transfers between devices  7.4 us (2%)
  other arithmetic  6.68 us (2%)
  between operations  3.8 us (1%)
    pallas_call x1, Pallas kernels, reduce_scatter(): pl.pallas_call(functools.partial(reduce_kernel, counts), out_shape=(*(jax...  111 us
    ppermute x5, waiting for transfers between devices, send(): return lax.ppermute(value, 'section', [(0, 1)] if steps > 0 else [(1, 0)])  86.8 us
    pallas_call x2, Pallas kernels, attn_fwd(): pl.pallas_call(functools.partial(attn_fwd_kernel, same), out_shape=(jax.S...  30 us
    pallas_call x2, Pallas kernels, ffn_fwd(): pl.pallas_call(ffn_fwd_kernel, out_shape=(jax.ShapeDtypeStruct((s, d), BF...  26.9 us
    pallas_call x2, Pallas kernels, ffn_bwd(): pl.pallas_call(functools.partial(ffn_bwd_kernel, extra), out_shape=(jax.S...  24 us
    another operation x2, loops' own time, cross(): return lax.cond(decoder, decode, encode)  12.1 us
    pallas_call x1, Pallas kernels, attn_bwd(): pl.pallas_call(attn_bwd_kernel, out_shape=(jax.ShapeDtypeStruct((s, d), F...  10.5 us
    unnamed x53, local copies, waits for them, and re-layouts  9.94 us
  transfers between devices with their start and end apart: 5, of which 2 were waited for; matrix products, arithmetic and copies ran while one was open for 2% of the time, Pallas kernels for 18%

profile of v3, /device:TPU:0, one launch (start us, length us, event | category | flops | bytes accessed | tf_op | source)
XLA Modules:
  0.0 352.3 jit_solution(7819525213875485393)
XLA Ops:
  4.0 9.8 %shard_map.263 = (bf16[256,2304]{1,0:T(8,128)(2,1)}, bf16[256,768]{1,0:T(8,128)(2,1)}, f32[256,768]{1,0:T(8,128)}, f32[256,768]{1,0:T(8,128)}, f32[256,128]{1,0:T(8,128)}, /*index=5*/f32[256,768]{1,0:T(8,128)S(1)}) custom-call(s32[1,1]{1,0:T(1,128)} %bitcast.12.len_ref, bf16[256,768]{1,0:T(8,128)(2,1)} %bitcast.77, bf16[256,768]{1,0:T(8,128)(2,1)} %bitcast.78, ...), custom_call_target="tpu_custom_call" | custom-call | tf_op jit(solution)/shard_map/pallas_call | solution.py:110
  13.9 9.8 %conditional.9 = ((bf16[256,768]{1,0:T(8,128)(2,1)}, bf16[256,3072]{1,0:T(8,128)(2,1)}, bf16[256,3072]{1,0:T(8,128)(2,1)}, f32[256,768]{1,0:T(8,128)}, f32[256,128]{1,0:T(8,128)})) conditional(s32[]{:T(128)} %convert_element_type.2, (f32[256,768]{1,0:T(8,128)S(1)}, bf16[768,3072]{1,0:T(8,128)(2,1)}, bf16[3072,768]{1,0:T(8,128)(2,1)}, ...), branch_computations={%region_0.1_spmd, %region_1.2_spmd} | conditional | bytes 8 | solution.py:815
  13.9 9.8 %branch_0_fun.11 = (bf16[256,768]{1,0:T(8,128)(2,1)}, bf16[256,3072]{1,0:T(8,128)(2,1)}, bf16[256,3072]{1,0:T(8,128)(2,1)}, f32[256,768]{1,0:T(8,128)}, f32[256,128]{1,0:T(8,128)}) custom-call(f32[256,768]{1,0:T(8,128)S(1)} %get-tuple-element.224.n_ref, bf16[768,3072]{1,0:T(8,128)(2,1)} %get-tuple-element.225.we_ref, ...), custom_call_target="tpu_custom_call" | custom-call | tf_op jit(solution)/shard_map/cond/branch_0_fun/pallas_call | solution.py:274
  26.9 20.2 %shard_map.264 = (bf16[640,2304]{1,0:T(8,128)(2,1)}, bf16[640,768]{1,0:T(8,128)(2,1)}, f32[640,768]{1,0:T(8,128)}, f32[640,768]{1,0:T(8,128)}, f32[640,128]{1,0:T(8,128)}, /*index=5*/f32[640,768]{1,0:T(8,128)S(1)}) custom-call(s32[1,1]{1,0:T(1,128)} %bitcast.8.len_ref.refs_0_, bf16[640,768]{1,0:T(8,128)(2,1)} %bitcast.73, bf16[640,768]{1,0:T(8,128)(2,1)} %bitcast.74, ...), custom_call_target="tpu_custom_call" | custom-call | tf_op jit(solution)/shard_map/pallas_call | solution.py:110
  47.9 17.4 %conditional.10 = ((bf16[640,768]{1,0:T(8,128)(2,1)}, bf16[640,3072]{1,0:T(8,128)(2,1)}, bf16[640,3072]{1,0:T(8,128)(2,1)}, f32[640,768]{1,0:T(8,128)}, f32[640,128]{1,0:T(8,128)})) conditional(s32[]{:T(128)} %convert_element_type.2, (f32[640,768]{1,0:T(8,128)S(1)}, bf16[768,3072]{1,0:T(8,128)(2,1)}, bf16[3072,768]{1,0:T(8,128)(2,1)}, ...), branch_computations={%region_2.3_spmd, %region_3.4_spmd} | conditional | bytes 8 | solution.py:815
  48.1 17.1 %branch_0_fun.12 = (bf16[640,768]{1,0:T(8,128)(2,1)}, bf16[640,3072]{1,0:T(8,128)(2,1)}, bf16[640,3072]{1,0:T(8,128)(2,1)}, f32[640,768]{1,0:T(8,128)}, f32[640,128]{1,0:T(8,128)}) custom-call(f32[640,768]{1,0:T(8,128)S(1)} %get-tuple-element.230.n_ref, bf16[768,3072]{1,0:T(8,128)(2,1)} %get-tuple-element.231.we_ref, ...), custom_call_target="tpu_custom_call" | custom-call | tf_op jit(solution)/shard_map/cond/branch_0_fun/pallas_call | solution.py:274
  65.3 2.2 collective-permute-start.1
  69.8 19.0 %collective-permute-done.1 = bf16[640,768]{1,0:T(8,128)(2,1)} collective-permute-done((bf16[640,768]{1,0:T(8,128)(2,1)}, bf16[640,768]{1,0:T(8,128)(2,1)}, u32[]{:S(2)}, u32[]{:S(2)}) %collective-permute-start.1) | collective-permute-done | bytes 983072 | tf_op jit(solution)/shard_map/ppermute | solution.py:818
  88.8 12.0 %conditional.13 = ((bf16[640,2304]{1,0:T(8,128)(2,1)}, bf16[640,768]{1,0:T(8,128)(2,1)}, f32[640,768]{1,0:T(8,128)}, f32[640,768]{1,0:T(8,128)}, f32[640,128]{1,0:T(8,128)}, /*index=5*/f32[640,768]{1,0:T(8,128)})) conditional(s32[]{:T(128)} %convert_element_type.2, () %tuple.92, (s32[1,1]{1,0:T(1,128)}, f32[640,768]{1,0:T(8,128)S(1)}, ...), branch_computations={%region_8.9_spmd, %region_9.10_spmd} | conditional | bytes 8 | solution.py:831
  100.9 7.0 %conditional.14 = ((bf16[640,3072]{1,0:T(8,128)(2,1)}, bf16[640,3072]{1,0:T(8,128)(2,1)}, bf16[640,768]{1,0:T(8,128)(2,1)}, bf16[640,2304]{1,0:T(8,128)(2,1)}, b...) conditional(s32[]{:T(128)} %convert_element_type.2, () %tuple.91, ...), branch_computations={%region_10.11_spmd, %region_11.12_spmd} | conditional | bytes 1310844 | solution.py:858
  109.2 1.8 select_bitcast_fusion.1
  111.0 1.4 add.21.refs_29_
  113.7 2.3 select_bitcast_fusion
  115.9 9.5 %conditional.15 = ((f32[256,768]{1,0:T(8,128)}, bf16[256,3072]{1,0:T(8,128)(2,1)}, bf16[256,768]{1,0:T(8,128)(2,1)}, f32[8,768]{1,0:T(8,128)}, f32[1,3072]{1,0:T(1,128)})) conditional(s32[]{:T(128)} %convert_element_type.2, (s32[1,1]{1,0:T(1,128)}, bf16[256,768]{1,0:T(8,128)(2,1)S(1)}, bf16[256,768]{1,0:T(8,128)(2,1)}, ...), branch_computations={%region_12.13_spmd, %region_13.14_spmd} | conditional | bytes 48 | solution.py:906
  115.9 9.5 %branch_0_fun.17 = (f32[256,768]{1,0:T(8,128)}, bf16[256,3072]{1,0:T(8,128)(2,1)}, bf16[256,768]{1,0:T(8,128)(2,1)}, f32[8,768]{1,0:T(8,128)}, f32[1,3072]{1,0:T(1,128)}) custom-call(s32[1,1]{1,0:T(1,128)} %get-tuple-element.321.len_ref, bf16[256,768]{1,0:T(8,128)(2,1)S(1)} %get-tuple-element.322.cot_ref, bf16[256,768]{1,0:T(8,128)(2,1)} %get-tuple-element.323.dm_ref, ...), custom_call_target="tpu_custom_call" | custom-call | tf_op jit(solution)/shard_map/cond/branch_0_fun/pallas_call | solution.py:324
  125.5 10.5 %shard_map.265 = (f32[256,768]{1,0:T(8,128)}, bf16[256,2304]{1,0:T(8,128)(2,1)}, bf16[256,768]{1,0:T(8,128)(2,1)}, bf16[8,128]{1,0:T(8,128)(2,1)}, f32[8,768]{1,0:T(8,128)}) custom-call(s32[1,1]{1,0:T(1,128)} %bitcast.12.len_ref, f32[256,768]{1,0:T(8,128)} %get-tuple-element.508.dn_ref, bf16[256,2304]{1,0:T(8,128)(2,1)} %get-tuple-element.509.qkv_hbm, ...), custom_call_target="tpu_custom_call" | custom-call | tf_op jit(solution)/shard_map/pallas_call | solution.py:225
  136.1 67.8 %collective-permute-done.3 = bf16[640,768]{1,0:T(8,128)(2,1)} collective-permute-done((bf16[640,768]{1,0:T(8,128)(2,1)}, bf16[640,768]{1,0:T(8,128)(2,1)}, u32[]{:S(2)}, u32[]{:S(2)}) %collective-permute-start.3) | collective-permute-done | bytes 983072 | tf_op jit(solution)/shard_map/ppermute | solution.py:818
  203.9 24.5 %conditional.16 = (f32[640,768]{1,0:T(8,128)}, bf16[640,3072]{1,0:T(8,128)(2,1)}, f32[8,768]{1,0:T(8,128)}, f32[1,3072]{1,0:T(1,128)}, bf16[8,2,2,2,2,48,384]{6,5,4,3,2,1,0:T(8,128)(2,1)}) conditional(s32[]{:T(128)} %convert_element_type.2, (s32[1,1]{1,0:T(1,128)}, bf16[640,768]{1,0:T(8,128)(2,1)}, bf16[640,768]{1,0:T(8,128)(2,1)}, ...), branch_computations={%region_14.15_spmd, %region_15.16_spmd} | conditional | flops 9216 | bytes 11907196 | solution.py:930
  204.1 14.6 %branch_0_fun.18 = (f32[640,768]{1,0:T(8,128)}, bf16[640,3072]{1,0:T(8,128)(2,1)}, bf16[640,768]{1,0:T(8,128)(2,1)}, f32[8,768]{1,0:T(8,128)}, f32[1,3072]{1,0:T(1,128)}) custom-call(s32[1,1]{1,0:T(1,128)} %get-tuple-element.334.len_ref, bf16[640,768]{1,0:T(8,128)(2,1)} %get-tuple-element.335.cot_ref, bf16[640,768]{1,0:T(8,128)(2,1)} %get-tuple-element.336.dm_ref, ...), custom_call_target="tpu_custom_call" | custom-call | tf_op jit(solution)/shard_map/cond/branch_0_fun/pallas_call | solution.py:324
  218.7 8.5 %branch_0_fun.19 = bf16[8,16,48,384]{3,2,1,0:T(8,128)(2,1)} custom-call(bf16[256,3072]{1,0:T(8,128)(2,1)} %get-tuple-element.349.refs_0_, bf16[640,3072]{1,0:T(8,128)(2,1)S(1)} %get-tuple-element.350.refs_1_, bf16[256,768]{1,0:T(8,128)(2,1)} %get-tuple-element.351.refs_2_, bf16[640,768]{1,0:T(8,128)(2,1)} %get-tuple-element.352.refs_3_), custom_call_target="tpu_custom_call" | custom-call | tf_op jit(solution)/shard_map/cond/branch_0_fun/pallas_call | solution.py:370
  228.4 111.4 %shard_map.266 = (f32[640,768]{1,0:T(8,128)}, f32[48,2304]{1,0:T(8,128)}, f32[48,768]{1,0:T(8,128)}, f32[48,3072]{1,0:T(8,128)}, f32[192,768]{1,0:T(8,128)}, /*i...) custom-call(s32[1,1]{1,0:T(1,128)} %bitcast.8.len_ref.refs_0_, ...), custom_call_target="tpu_custom_call" | custom-call | tf_op jit(solution)/shard_map/pallas_call | solution.py:726
  339.8 1.3 slice_reduce_fusion
  341.9 1.4 fusion
  345.2 3.0 copy.161
  (81 shorter events, 17.3 us)
Async XLA Ops:
  2.7 44.4 %copy-start.7 = (f32[1,6,768]{2,1,0:T(8,128)}, f32[1,6,768]{2,1,0:T(8,128)S(1)}, u32[]{:S(2)}) copy-start(f32[1,6,768]{2,1,0:T(8,128)S(1)} %copy.42) | copy-start | bytes 55300
  4.0 9.8 %copy-start.6 = (f32[1,2,768]{2,1,0:T(2,128)S(1)}, f32[1,2,768]{2,1,0:T(2,128)}, u32[]{:S(2)}) copy-start(f32[1,2,768]{2,1,0:T(2,128)} %param.46) | copy-start | bytes 18436
  4.0 9.8 %copy-start.15 = (f32[1,3072]{1,0:T(1,128)S(1)}, f32[1,3072]{1,0:T(1,128)}, u32[]{:S(2)}) copy-start(f32[1,3072]{1,0:T(1,128)} %param.44) | copy-start | bytes 36868
  13.8 111.6 %copy-start.1 = (f32[256,768]{1,0:T(8,128)}, f32[256,768]{1,0:T(8,128)S(1)}, u32[]{:S(2)}) copy-start(f32[256,768]{1,0:T(8,128)S(1)} %get-tuple-element.483.refs_18_) | copy-start | bytes 2359300
  13.8 11.1 %copy-start.28 = (s32[2,1]{0,1:T(1,128)S(1)}, s32[2,1]{0,1:T(1,128)}, u32[]{:S(2)}) copy-start(s32[2,1]{0,1:T(1,128)} %param.38) | copy-start | bytes 28
  23.7 23.5 %collective-permute-start = (bf16[256,768]{1,0:T(8,128)(2,1)}, bf16[256,768]{1,0:T(8,128)(2,1)S(1)}, u32[]{:S(2)}, u32[]{:S(2)}) collective-permute-start(bf16[256,768]{1,0:T(8,128)(2,1)} %get-tuple-element.478), channel_id=1, source_target_pairs={{0,16},{1,17},{2,18},{3,19},{4,20},{5,21},{6,22},{7,23},{8,24},{9,... | collective-permute-start | bytes 1179656 | tf_op jit(solution)/shard_map/ppermute | solution.py:818
  47.1 78.3 %copy-start = (f32[640,768]{1,0:T(8,128)}, f32[640,768]{1,0:T(8,128)S(1)}, u32[]{:S(2)}) copy-start(f32[640,768]{1,0:T(8,128)S(1)} %get-tuple-element.492.refs_19_) | copy-start | bytes 5898244
  47.1 20.4 %copy-start.27 = (f32[768]{0:T(1024)S(1)}, f32[768]{0:T(1024)}, u32[]{:S(2)}) copy-start(f32[768]{0:T(1024)} %param.49) | copy-start | bytes 9220
  65.3 23.5 %collective-permute-start.1 = (bf16[640,768]{1,0:T(8,128)(2,1)}, bf16[640,768]{1,0:T(8,128)(2,1)}, u32[]{:S(2)}, u32[]{:S(2)}) collective-permute-start(bf16[640,768]{1,0:T(8,128)(2,1)} %get-tuple-element.482), channel_id=1, source_target_pairs={{0,16},{1,17},{2,18},{3,19},{4,20},{5,21},{6,22},{7,23},{8,24},{9,... | collective-permute-start | bytes 2949128 | tf_op jit(solution)/shard_map/ppermute | solution.py:818
  68.5 32.3 %collective-permute-start.2 = (bf16[256,768]{1,0:T(8,128)(2,1)}, bf16[256,768]{1,0:T(8,128)(2,1)}, u32[]{:S(2)}, u32[]{:S(2)}) collective-permute-start(bf16[256,768]{1,0:T(8,128)(2,1)} %get-tuple-element.491), channel_id=1, source_target_pairs={{16,0},{17,1},{18,2},{19,3},{20,4},{21,5},{22,6},{23,7},{24,8},{25... | collective-permute-start | bytes 1179656 | tf_op jit(solution)/shard_map/ppermute | solution.py:818
  107.9 96.0 %collective-permute-start.3 = (bf16[640,768]{1,0:T(8,128)(2,1)}, bf16[640,768]{1,0:T(8,128)(2,1)}, u32[]{:S(2)}, u32[]{:S(2)}) collective-permute-start(bf16[640,768]{1,0:T(8,128)(2,1)} %get-tuple-element.502), channel_id=1, source_target_pairs={{16,0},{17,1},{18,2},{19,3},{20,4},{21,5},{22,6},{23,7},{24,8},{25... | collective-permute-start | bytes 2949128 | tf_op jit(solution)/shard_map/ppermute | solution.py:818
  109.2 6.8 %copy-start.18 = (f32[256,128]{1,0:T(8,128)S(1)}, f32[256,128]{1,0:T(8,128)}, u32[]{:S(2)}) copy-start(f32[256,128]{1,0:T(8,128)} %get-tuple-element.506) | copy-start | bytes 393220
  112.4 116.0 %collective-permute-start.4 = (f32[8,768]{1,0:T(8,128)}, f32[8,768]{1,0:T(8,128)}, u32[]{:S(2)}, u32[]{:S(2)}) collective-permute-start(f32[8,768]{1,0:T(8,128)} %add.21.refs_29_), channel_id=1, source_target_pairs={{16,0},{17,1},{18,2},{19,3},{20,4},{21,5},{22,6},{23,7},{24,8},{25... | collective-permute-start | bytes 73736 | tf_op jit(solution)/shard_map/ppermute | solution.py:818
  125.5 78.4 %copy-start.2 = (bf16[640,3072]{1,0:T(8,128)(2,1)S(1)}, bf16[640,3072]{1,0:T(8,128)(2,1)}, u32[]{:S(2)}) copy-start(bf16[640,3072]{1,0:T(8,128)(2,1)} %get-tuple-element.522) | copy-start | bytes 11796484
  125.5 78.4 %copy-start.19 = (f32[8,768]{1,0:T(8,128)S(1)}, f32[8,768]{1,0:T(8,128)}, u32[]{:S(2)}) copy-start(f32[8,768]{1,0:T(8,128)} %get-tuple-element.524) | copy-start | bytes 73732
  125.5 78.4 %copy-start.20 = (f32[8,768]{1,0:T(8,128)S(1)}, f32[8,768]{1,0:T(8,128)}, u32[]{:S(2)}) copy-start(f32[8,768]{1,0:T(8,128)} %get-tuple-element.525) | copy-start | bytes 73732
  125.5 78.4 %copy-start.22 = (f32[8,768]{1,0:T(8,128)S(1)}, f32[8,768]{1,0:T(8,128)}, u32[]{:S(2)}) copy-start(f32[8,768]{1,0:T(8,128)} %get-tuple-element.519) | copy-start | bytes 73732
  125.5 78.4 %copy-start.23 = (f32[1,3072]{1,0:T(1,128)S(1)}, f32[1,3072]{1,0:T(1,128)}, u32[]{:S(2)}) copy-start(f32[1,3072]{1,0:T(1,128)} %get-tuple-element.526) | copy-start | bytes 36868
  125.5 78.4 %copy-start.24 = (f32[1,3072]{1,0:T(1,128)S(1)}, f32[1,3072]{1,0:T(1,128)}, u32[]{:S(2)}) copy-start(f32[1,3072]{1,0:T(1,128)} %get-tuple-element.527) | copy-start | bytes 36868
  125.5 78.4 %copy-start.26 = (f32[1,3072]{1,0:T(1,128)S(1)}, f32[1,3072]{1,0:T(1,128)}, u32[]{:S(2)}) copy-start(f32[1,3072]{1,0:T(1,128)} %get-tuple-element.520) | copy-start | bytes 36868
  218.7 8.5 %copy-start.25 = (f32[1,3072]{1,0:T(1,128)S(1)}, f32[1,3072]{1,0:T(1,128)}, u32[]{:S(2)}) copy-start(f32[1,3072]{1,0:T(1,128)} %get-tuple-element.348) | copy-start | bytes 36868 | tf_op jit(solution)/shard_map/cond
  218.7 9.1 %copy-start.21 = (f32[8,768]{1,0:T(8,128)S(1)}, f32[8,768]{1,0:T(8,128)}, u32[]{:S(2)}) copy-start(f32[8,768]{1,0:T(8,128)} %get-tuple-element.346) | copy-start | bytes 73732 | tf_op jit(solution)/shard_map/cond
  345.2 3.8 %copy-start.16 = (f32[48,768]{1,0:T(8,128)S(1)}, f32[48,768]{1,0:T(8,128)}, u32[]{:S(2)}) copy-start(f32[48,768]{1,0:T(8,128)} %get-tuple-element.559) | copy-start | bytes 442372
  345.2 4.5 %copy-start.10 = (f32[48,3072]{1,0:T(8,128)S(1)}, f32[48,3072]{1,0:T(8,128)}, u32[]{:S(2)}) copy-start(f32[48,3072]{1,0:T(8,128)} %get-tuple-element.560) | copy-start | bytes 1769476
  (5 other events, 10.1 us)
